TPU v7x, 512 devices: a whole 4x4x16 slice. The times are simulated.
512 devices in a mesh: row: 16 (over x, z_hi, core), col: 32 (over z_lo, y).
Axes of the slice: x: 4, y: 4, z: 16 (z_hi: 2, z_lo: 8; z = z_hi * 8 + z_lo), core: 2. Of those that a mesh axis runs over, the one named last changes fastest.
Arguments:
- density: float32 [8192, 8192], P('row', 'col'), may hold values from -0.4375 to 0.4375
- occupancy: int32 [64, 64], P('row', 'col'), may hold values from 0 to 1, as said below
Outputs:
- purified: float32 [8192, 8192], P('row', 'col')
Inputs may be any that keep to these rules, and one draw needn't show every extreme that they name: `occupancy`: 1 marks an occupied 128 x 128 tile, 0 an empty one; every diagonal tile is occupied.
All inputs are finite; a program needn't handle non-finite values.
Results may differ from a plain program's by a relative error of at most 0.0001.
Values sent between devices are 32-bit elements; how exact they have to be, the bound alone decides.
No kernel may reach another device: no remote copies, remote signals or barrier semaphores. Data moves between devices by JAX's collectives and lax.ppermute only.
A program may use at most 64 MiB of HBM per device.

v0:
```python
import jax
import jax.numpy as jnp
from jax import lax
from jax.sharding import PartitionSpec as P

SECTIONS = 3


def from_root(block, axis, owner):
    block = jnp.where(lax.axis_index(axis) == owner, block, jnp.zeros_like(block))
    return lax.psum(block, axis)


def passed_along(value, axis, by):
    size = lax.axis_size(axis)
    return lax.ppermute(value, axis, [(i, (i + by) % size) for i in range(size)])


def tile_mask(values, occupancy):
    row_total, col_total = values.shape
    tile_rows, tile_cols = occupancy.shape
    shaped = values.reshape(tile_rows, row_total // tile_rows, tile_cols, col_total // tile_cols)
    weights = occupancy.astype(jnp.float32)[:, None, :, None]
    return (shaped * weights).reshape(row_total, col_total)


def left_blocks(masked):
    row_count = lax.axis_size("row")
    row_index = lax.axis_index("row")
    left_list = []
    for section_index in range(SECTIONS):
        owner_block = (row_index + section_index) % row_count
        halves = []
        for half_index in range(2):
            halves.append(from_root(masked, "col", 2 * owner_block + half_index))
        left_list.append(jnp.concatenate(halves, axis=1))
    return left_list


def right_rows(factor):
    right_list = [factor]
    current = factor
    for section_index in range(1, SECTIONS):
        current = passed_along(current, "row", -1)
        right_list.append(current)
    return right_list


def windowed(left_list, right_list):
    accum = jnp.zeros((left_list[0].shape[0], right_list[0].shape[1]), jnp.float32)
    for section_index in range(SECTIONS):
        accum = accum + jnp.dot(
            left_list[section_index],
            right_list[section_index],
            precision=lax.Precision.HIGHEST,
            preferred_element_type=jnp.float32,
        )
    return accum


def per_device(density, occupancy):
    masked = tile_mask(density, occupancy)
    left_list = left_blocks(masked)
    square_term = tile_mask(windowed(left_list, right_rows(masked)), occupancy)
    cube_term = tile_mask(windowed(left_list, right_rows(square_term)), occupancy)
    return 3.0 * square_term - 2.0 * cube_term


def solution(mesh):
    in_specs = (P("row", "col"), P("row", "col"))
    out_specs = P("row", "col")
    return jax.shard_map(
        per_device, mesh=mesh, in_specs=in_specs, out_specs=out_specs, check_vma=False
    )
```

profile of v0, /device:TPU:6, one launch (start us, length us, event | category | flops | bytes accessed | tf_op | source)
XLA Modules:
  0.0 567.0 jit_solution(18337542183941033267)
XLA Ops:
  6.5 0.0 copy-start
  6.5 0.0 all-reduce.3.cloned.1.call-start
  6.5 0.7 convert_element_type.2
  7.3 0.1 copy.3
  7.4 0.2 mul.50
  7.6 0.0 copy-done
  7.6 0.9 broadcast_select_fusion
  8.5 1.6 broadcast_select_fusion.1
  10.1 0.0 all-reduce.3.cloned.1.call-update
  10.1 15.4 %collective-permute-start = (f32[512,256]{1,0:T(8,128)S(1)}, f32[512,256]{1,0:T(8,128)S(1)}, u32[]{:S(2)}, u32[]{:S(2)}) collective-permute-start(f32[512,256]{1,0:T(8,128)S(1)} %get-tuple-element.12), channel_id=1, source_target_pairs={{0,480},{32,0},{64,32},{96,64},{128,96},{160,128},{192,160},{224,1... | collective-permute-start | bytes 1572872 | tf_op jit(solution)/shard_map/ppermute | solution.py:16
  25.5 22.5 %collective-permute-done = f32[512,256]{1,0:T(8,128)S(1)} collective-permute-done((f32[512,256]{1,0:T(8,128)S(1)}, f32[512,256]{1,0:T(8,128)S(1)}, u32[]{:S(2)}, u32[]{:S(2)}) %collective-permute-start) | collective-permute-done | bytes 524320 | tf_op jit(solution)/shard_map/ppermute | solution.py:16
  48.1 13.5 %collective-permute-start.1 = (f32[512,256]{1,0:T(8,128)S(1)}, f32[512,256]{1,0:T(8,128)S(1)}, u32[]{:S(2)}, u32[]{:S(2)}) collective-permute-start(f32[512,256]{1,0:T(8,128)S(1)} %collective-permute-done), channel_id=1, source_target_pairs={{0,480},{32,0},{64,32},{96,64},{128,96},{160,128},{192,160},{224,1... | collective-permute-start | bytes 1572872 | tf_op jit(solution)/shard_map/ppermute | solution.py:16
  61.6 452.3 %all-reduce.3.cloned.1.call-done = (f32[512,256]{1,0:T(8,128)}, f32[512,256]{1,0:T(8,128)}, f32[512,256]{1,0:T(8,128)}, f32[512,256]{1,0:T(8,128)}, f32[512,256]{1,0:T(8,128)}, /*index=5*/f32[512,256]{1,0:T(8,128)}) async-done(((f32[512,256]{1,0:T(8,128)}, f32[512,256]{1,0:T(8,128)}, f32[512,256]{1,0:T(8,128)}, f32[512,256]{1,0:T(8,128)}, f32[512,256]{1,0:T(8,128)}, /*index=5*/f32[512,256]{1,0:T(8,128)}), ...) | async-done | bytes 3145744 | tf_op jit(solution)/shard_map/psum | solution.py:11
  513.9 0.0 copy-start.3
  513.9 1.2 constant_dynamic-update-slice_fusion.5
  515.0 0.0 copy-done.3
  515.1 0.0 copy-start.2
  515.1 0.1 constant_dynamic-update-slice_fusion.1
  515.1 1.0 copy-done.2
  516.1 0.0 copy-start.1
  516.1 0.1 constant_dynamic-update-slice_fusion.3
  516.2 1.0 copy-done.1
  517.2 0.0 copy-start.4
  517.2 0.0 copy-start.5
  517.2 0.1 constant_dynamic-update-slice_fusion.4
  517.2 1.0 copy-done.4
  518.2 0.2 copy-done.5
  518.4 0.1 constant_dynamic-update-slice_fusion
  518.5 1.0 fusion.3
  519.5 1.0 convolution_add_fusion.3
  520.5 0.0 collective-permute-done.1
  520.5 1.0 fusion
  521.5 1.9 collective-permute-start.2
  523.4 14.7 %collective-permute-done.2 = f32[512,256]{1,0:T(8,128)S(1)} collective-permute-done((f32[512,256]{1,0:T(8,128)S(1)}, f32[512,256]{1,0:T(8,128)S(1)}, u32[]{:S(2)}, u32[]{:S(2)}) %collective-permute-start.2) | collective-permute-done | bytes 524320 | tf_op jit(solution)/shard_map/ppermute | solution.py:16
  538.2 13.5 %collective-permute-start.3 = (f32[512,256]{1,0:T(8,128)S(1)}, f32[512,256]{1,0:T(8,128)S(1)}, u32[]{:S(2)}, u32[]{:S(2)}) collective-permute-start(f32[512,256]{1,0:T(8,128)S(1)} %collective-permute-done.2), channel_id=1, source_target_pairs={{0,480},{32,0},{64,32},{96,64},{128,96},{160,128},{192,160},{224,1... | collective-permute-start | bytes 1572872 | tf_op jit(solution)/shard_map/ppermute | solution.py:16
  551.7 1.0 fusion.4
  552.7 1.0 convolution_add_fusion.1
  553.7 4.7 collective-permute-done.3
  558.3 1.8 multiply_subtract_fusion
Async XLA Ops:
  6.5 1.1 copy-start
  6.5 507.3 %all-reduce.3.cloned.1.call-start = ((), (), s32[]{:S(2)}) async-start(), calls=%async_computation | async-start | bytes 6291456 | tf_op jit(solution)/shard_map/psum | solution.py:11
  10.1 38.0 %collective-permute-start = (f32[512,256]{1,0:T(8,128)S(1)}, f32[512,256]{1,0:T(8,128)S(1)}, u32[]{:S(2)}, u32[]{:S(2)}) collective-permute-start(f32[512,256]{1,0:T(8,128)S(1)} %get-tuple-element.12), channel_id=1, source_target_pairs={{0,480},{32,0},{64,32},{96,64},{128,96},{160,128},{192,160},{224,1... | collective-permute-start | bytes 1572872 | tf_op jit(solution)/shard_map/ppermute | solution.py:16
  48.1 472.4 %collective-permute-start.1 = (f32[512,256]{1,0:T(8,128)S(1)}, f32[512,256]{1,0:T(8,128)S(1)}, u32[]{:S(2)}, u32[]{:S(2)}) collective-permute-start(f32[512,256]{1,0:T(8,128)S(1)} %collective-permute-done), channel_id=1, source_target_pairs={{0,480},{32,0},{64,32},{96,64},{128,96},{160,128},{192,160},{224,1... | collective-permute-start | bytes 1572872 | tf_op jit(solution)/shard_map/ppermute | solution.py:16
  513.9 1.2 copy-start.3
  515.1 1.0 copy-start.2
  516.1 1.0 copy-start.1
  517.2 1.0 copy-start.4
  517.2 1.2 copy-start.5
  521.5 16.7 %collective-permute-start.2 = (f32[512,256]{1,0:T(8,128)S(1)}, f32[512,256]{1,0:T(8,128)S(1)}, u32[]{:S(2)}, u32[]{:S(2)}) collective-permute-start(f32[512,256]{1,0:T(8,128)S(1)} %fusion), channel_id=1, source_target_pairs={{0,480},{32,0},{64,32},{96,64},{128,96},{160,128},{192,160},{224,1... | collective-permute-start | bytes 1572872 | tf_op jit(solution)/shard_map/ppermute | solution.py:16
  538.2 20.2 %collective-permute-start.3 = (f32[512,256]{1,0:T(8,128)S(1)}, f32[512,256]{1,0:T(8,128)S(1)}, u32[]{:S(2)}, u32[]{:S(2)}) collective-permute-start(f32[512,256]{1,0:T(8,128)S(1)} %collective-permute-done.2), channel_id=1, source_target_pairs={{0,480},{32,0},{64,32},{96,64},{128,96},{160,128},{192,160},{224,1... | collective-permute-start | bytes 1572872 | tf_op jit(solution)/shard_map/ppermute | solution.py:16
Sparse Core Ops, SparseCore 0:
  10.7 503.1 all-reduce.2
where the time goes:
time: 568 us; the launch traced here: 567 us
  waiting for transfers between devices  494 us (87%)
  starting transfers between devices  44.4 us (8%)
  between operations  13.5 us (2%)
  matrix products  6.75 us (1%)
    psum x1, waiting for transfers between devices, from_root(): return lax.psum(block, axis)  452 us
    ppermute x4, starting transfers between devices, passed_along(): lax.ppermute(value, axis, [(i, (i + by) % size) for i in range(size)])  44.4 us
    ppermute x4, waiting for transfers between devices, passed_along(): lax.ppermute(value, axis, [(i, (i + by) % size) for i in range(size)])  42 us
  transfers between devices with their start and end apart: 5, of which 4 were waited for; matrix products, arithmetic and copies ran while one was open for 1% of the time, Pallas kernels for 0%

commit v1 on v0

v1 whole, which is shorter than its diff:
```python
import jax
import jax.numpy as jnp
from jax import lax
from jax.sharding import PartitionSpec as P

NX, NY, NZ = 4, 4, 8


def coords():
    for x in range(NX):
        for zh in range(2):
            for core in range(2):
                for zl in range(NZ):
                    for y in range(NY):
                        yield x, zh, core, zl, y


def linear(x, zh, core, zl, y):
    return ((x * 2 + zh) * 2 + core) * (NZ * NY) + zl * NY + y


def move(value, rule):
    pairs = []
    for at in coords():
        to = rule(*at)
        if to is not None:
            pairs.append((linear(*at), linear(*to)))
    return lax.ppermute(value, ("row", "col"), pairs)


def half_of(x, zh, core, zl, y):
    row = (x * 2 + zh) * 2 + core
    return (zl * NY + y - 2 * row) % (NZ * NY)


def owner(*at):
    return half_of(*at) < 6


def prev_group(x, zh):
    q = (x * 2 + zh - 1) % (2 * NX)
    return q // 2, q % 2


def tile_mask(values, occupancy):
    row_total, col_total = values.shape
    tile_rows, tile_cols = occupancy.shape
    shaped = values.reshape(tile_rows, row_total // tile_rows, tile_cols, col_total // tile_cols)
    weights = occupancy.astype(jnp.float32)[:, None, :, None]
    return (shaped * weights).reshape(row_total, col_total)


def after(value, other):
    return lax.optimization_barrier((value, other))[0]


def per_device(density, occupancy):
    row, col = lax.axis_index("row"), lax.axis_index("col")
    core, zh = row % 2, (row // 2) % 2
    zl, y = col // NY, col % NY
    masked = tile_mask(density, occupancy)

    def from_plane(flip, known):
        def rule(x, zh, core, zl, y):
            for mask in known:
                if owner(x, zh, core, zl ^ mask, y):
                    return x, zh, core, zl ^ flip, y
            return None

        return rule

    is_owner = (col - 2 * row) % (NZ * NY) < 6
    is_owner4 = ((zl ^ 4) * NY + y - 2 * row) % (NZ * NY) < 6
    got = move(masked, from_plane(4, (0,)))
    held = jnp.where(is_owner, masked, got)
    got = move(held, from_plane(2, (0, 4)))
    held = jnp.where(is_owner | is_owner4, held, got)
    got = move(held, from_plane(1, (0, 4, 2, 6)))
    mine_full = (zl % 2) == ((zh + core) % 2)
    full = jnp.where(mine_full, held, got)
    part = jnp.where(mine_full, got, held)

    def far(x, zh, core, zl, y):
        return (*prev_group(x, zh), core, zl, y)

    def partner(x, zh, core, zl, y):
        return x, zh, 1 - core, zl, y

    def right_rows(value, anchor=None):
        two = move(value if anchor is None else after(value, anchor), far)
        one = move(jnp.where(core == 0, two, value), partner)
        return jnp.concatenate([value, one, two])

    right = right_rows(masked, got)

    def along(step):
        return lambda x, zh, core, zl, y: (x, zh, core, zl, (y + step) % NY)

    def swap(x, zh, core, zl, y):
        return x, zh, core, zl, y ^ 1

    def part_out(x, zh, core, zl, y):
        return (x, zh, core, zl, 3 - y) if y // 2 == core else None

    def part_swap(x, zh, core, zl, y):
        return (x, zh, core, zl, y ^ 1) if y // 2 == core else None

    def part_over(x, zh, core, zl, y):
        return (x, zh, core, zl, 3 - y) if y // 2 == core else None

    below = move(full, along(1))
    above = move(full, along(-1))
    part_a = move(part, part_out)
    part_b = move(part, part_swap)
    across = move(jnp.where(y % 2 == 0, below, above), swap)
    part_c = move(part_b, part_over)
    has_part = (y // 2) == core
    part_near = jnp.where(has_part, part, part_a)
    part_far = jnp.where(has_part, part_b, part_c)
    near_y = jnp.where(has_part, y, 3 - y)

    full_of = lambda who: who % NY + 2 * core
    part_of = lambda who: jnp.where(core == 0, 4 + who, who - 2)
    lefts = [
        (full, full_of(y)),
        (below, full_of(y + NY - 1)),
        (above, full_of(y + 1)),
        (across, full_of(y + 2)),
        (part_near, part_of(near_y)),
        (part_far, part_of(near_y ^ 1)),
    ]

    def windowed(right):
        width = right.shape[1]
        accum = 0.0
        for left, half in lefts:
            rows = lax.dynamic_slice(right, (half * width, 0), (width, width))
            accum = accum + jnp.dot(
                left, rows, precision=lax.Precision.HIGHEST, preferred_element_type=jnp.float32
            )
        return accum

    square_term = tile_mask(windowed(right), occupancy)
    cube_term = tile_mask(windowed(right_rows(square_term)), occupancy)
    return 3.0 * square_term - 2.0 * cube_term


def solution(mesh):
    spec = P("row", "col")
    return jax.shard_map(
        per_device, mesh=mesh, in_specs=(spec, spec), out_specs=spec, check_vma=False
    )
```

time: 568 us -> 213 us (0.38)
  waiting for transfers between devices: 494 us -> 169 us
  starting transfers between devices: 44.4 us -> 27 us
  between operations: 13.5 us -> 0.57 us
    psum x1 -> x0, waiting for transfers between devices: 452 us -> none  [from_root(): return lax.psum(block, axis)]
    ppermute x4 -> x13, waiting for transfers between devices: 42 us -> 169 us  [move(): return lax.ppermute(value, ('row', 'col'), pairs)]
    ppermute x4 -> x13, starting transfers between devices: 44.4 us -> 27 us  [move(): return lax.ppermute(value, ('row', 'col'), pairs)]
  transfers between devices with their start and end apart: 5 -> 13, of which waited for: 4 -> 6; matrix products, arithmetic and copies ran while one was open for 1% -> 3% of each run, Pallas kernels for 0% -> 0%
where the time goes in v1:
time: 213 us; the launch traced here: 212 us
  waiting for transfers between devices  169 us (79%)
  starting transfers between devices  27 us (13%)
  matrix products  10.1 us (5%)
  other arithmetic  5.45 us (3%)
    ppermute x13, waiting for transfers between devices, move(): return lax.ppermute(value, ('row', 'col'), pairs)  169 us
    ppermute x13, starting transfers between devices, move(): return lax.ppermute(value, ('row', 'col'), pairs)  27 us
    dot_general x12, matrix products, windowed(): jnp.dot(left, rows, precision=lax.Precision.HIGHEST, preferred_element_ty...  10.1 us
  transfers between devices with their start and end apart: 13, of which 6 were waited for; matrix products, arithmetic and copies ran while one was open for 3% of the time, Pallas kernels for 0%

profile of v1, /device:TPU:6, one launch (start us, length us, event | category | flops | bytes accessed | tf_op | source)
XLA Modules:
  0.0 212.3 jit_solution(323000554078656683)
XLA Ops:
  0.0 0.7 convert_element_type.2
  0.7 0.1 copy.3
  0.8 0.2 mul.76
  1.0 1.1 bitcast_multiply_fusion
  2.1 0.7 collective-permute-start
  2.8 0.0 collective-permute-done
  2.8 0.1 broadcast_select_fusion.5
  2.9 1.3 collective-permute-start.1
  4.3 47.9 %collective-permute-done.1 = f32[512,256]{1,0:T(8,128)S(1)} collective-permute-done((f32[512,256]{1,0:T(8,128)S(1)}, f32[512,256]{1,0:T(8,128)S(1)}, u32[]{:S(2)}, u32[]{:S(2)}) %collective-permute-start.1) | collective-permute-done | bytes 524320 | tf_op jit(solution)/shard_map/ppermute | solution.py:28
  52.2 0.1 broadcast_select_fusion.6
  52.2 1.9 collective-permute-start.2
  54.2 44.8 %collective-permute-done.2 = f32[512,256]{1,0:T(8,128)S(1)} collective-permute-done((f32[512,256]{1,0:T(8,128)S(1)}, f32[512,256]{1,0:T(8,128)S(1)}, u32[]{:S(2)}, u32[]{:S(2)}) %collective-permute-start.2) | collective-permute-done | bytes 524320 | tf_op jit(solution)/shard_map/ppermute | solution.py:28
  99.0 1.9 collective-permute-start.3
  101.0 0.1 broadcast_select_fusion.8
  101.0 3.5 %collective-permute-start.5 = (f32[512,256]{1,0:T(8,128)S(1)}, f32[512,256]{1,0:T(8,128)S(1)}, u32[]{:S(2)}, u32[]{:S(2)}) collective-permute-start(f32[512,256]{1,0:T(8,128)S(1)} %get-tuple-element.7), channel_id=1, source_target_pairs={{0,1},{1,2},{2,3},{3,0},{4,5},{5,6},{6,7},{7,4},{8,9},{9,10},{10,1... | collective-permute-start | bytes 1572872 | tf_op jit(solution)/shard_map/ppermute | solution.py:28
  104.5 3.6 %collective-permute-start.6 = (f32[512,256]{1,0:T(8,128)S(1)}, f32[512,256]{1,0:T(8,128)S(1)}, u32[]{:S(2)}, u32[]{:S(2)}) collective-permute-start(f32[512,256]{1,0:T(8,128)S(1)} %get-tuple-element.7), channel_id=1, source_target_pairs={{0,3},{1,0},{2,1},{3,2},{4,7},{5,4},{6,5},{7,6},{8,11},{9,8},{10,9... | collective-permute-start | bytes 1572872 | tf_op jit(solution)/shard_map/ppermute | solution.py:28
  108.1 2.3 %collective-permute-start.9 = (f32[512,256]{1,0:T(8,128)S(1)}, f32[512,256]{1,0:T(8,128)}, u32[]{:S(2)}, u32[]{:S(2)}) collective-permute-start(f32[512,256]{1,0:T(8,128)S(1)} %get-tuple-element.8), channel_id=1, source_target_pairs={{0,1},{1,0},{4,5},{5,4},{8,9},{9,8},{12,13},{13,12},{16,17},{17,16... | collective-permute-start | bytes 1572872 | tf_op jit(solution)/shard_map/ppermute | solution.py:28
  110.4 13.8 %collective-permute-done.3 = f32[512,256]{1,0:T(8,128)} collective-permute-done((f32[512,256]{1,0:T(8,128)S(1)}, f32[512,256]{1,0:T(8,128)}, u32[]{:S(2)}, u32[]{:S(2)}) %collective-permute-start.3) | collective-permute-done | bytes 524320 | tf_op jit(solution)/shard_map/ppermute | solution.py:28
  124.2 1.9 broadcast_select_fusion.4
  126.1 1.9 collective-permute-start.4
  128.2 1.3 collective-permute-start.8
  129.5 0.0 collective-permute-done.5
  129.5 0.1 broadcast_select_fusion.2
  129.6 3.5 %collective-permute-start.7 = (f32[512,256]{1,0:T(8,128)S(1)}, f32[512,256]{1,0:T(8,128)S(1)}, u32[]{:S(2)}, u32[]{:S(2)}) collective-permute-start(f32[512,256]{1,0:T(8,128)S(1)} %broadcast_select_fusion.2), channel_id=1, source_target_pairs={{0,1},{1,0},{2,3},{3,2},{4,5},{5,4},{6,7},{7,6},{8,9},{9,8},{10,11... | collective-permute-start | bytes 1572872 | tf_op jit(solution)/shard_map/ppermute | solution.py:28
  133.1 1.3 collective-permute-start.10
  134.4 0.0 collective-permute-done.4
  134.5 1.3 pad_maximum_fusion
  135.8 0.6 fusion.26
  136.4 0.6 fusion.24
  136.9 0.0 collective-permute-done.8
  137.0 0.6 fusion.20
  137.6 8.2 %collective-permute-done.7 = f32[512,256]{1,0:T(8,128)S(1)} collective-permute-done((f32[512,256]{1,0:T(8,128)S(1)}, f32[512,256]{1,0:T(8,128)S(1)}, u32[]{:S(2)}, u32[]{:S(2)}) %collective-permute-start.7) | collective-permute-done | bytes 524320 | tf_op jit(solution)/shard_map/ppermute | solution.py:28
  145.8 0.6 fusion.22
  146.4 0.6 fusion.8
  147.0 0.0 collective-permute-done.10
  147.0 1.7 fusion.5
  148.7 1.9 collective-permute-start.11
  150.6 52.2 %collective-permute-done.11 = f32[512,256]{1,0:T(8,128)S(1)} collective-permute-done((f32[512,256]{1,0:T(8,128)S(1)}, f32[512,256]{1,0:T(8,128)S(1)}, u32[]{:S(2)}, u32[]{:S(2)}) %collective-permute-start.11) | collective-permute-done | bytes 524320 | tf_op jit(solution)/shard_map/ppermute | solution.py:28
  202.8 0.1 broadcast_select_fusion.3
  202.8 1.9 collective-permute-start.12
  204.8 1.9 collective-permute-done.12
  206.7 0.1 pad_maximum_fusion.1
  206.8 0.6 fusion.16
  207.4 0.6 fusion.14
  208.0 0.6 fusion.12
  208.5 0.6 fusion.10
  209.2 0.6 fusion.4
  209.8 2.5 %multiply_subtract_fusion = f32[512,256]{1,0:T(8,128)} fusion(f32[512,256]{1,0:T(8,128)S(1)} %fusion.5, f32[64,8,2,128]{3,2,1,0:T(2,128)S(1)} %bitcast.18, f32[512,256]{1,0:T(8,128)S(1)} %fusion.4, f32[1536,256]{1,0:T(8,128)S(1)} %pad_maximum_fusion.1, s32[]{:T(128)S(6)} %select_n.181, f32[512,256]{1,0:T(8,128)} %collective-permute-done.9, ...), kind=kOutput, calls=%fused_computation.16 | convolution fusion | flops 403439616 | bytes 3407877 | tf_op jit(solution)/shard_map/dot_general | solution.py:138
  (2 shorter events, 0.0 us)
Async XLA Ops:
  2.1 0.7 collective-permute-start
  2.9 49.3 %collective-permute-start.1 = (f32[512,256]{1,0:T(8,128)S(1)}, f32[512,256]{1,0:T(8,128)S(1)}, u32[]{:S(2)}, u32[]{:S(2)}) collective-permute-start(f32[512,256]{1,0:T(8,128)S(1)} %broadcast_select_fusion.5), channel_id=1, source_target_pairs={{0,8},{1,9},{2,10},{3,11},{4,12},{5,13},{16,24},{17,25},{18,26},{1... | collective-permute-start | bytes 1572872 | tf_op jit(solution)/shard_map/ppermute | solution.py:28
  52.2 46.7 %collective-permute-start.2 = (f32[512,256]{1,0:T(8,128)S(1)}, f32[512,256]{1,0:T(8,128)S(1)}, u32[]{:S(2)}, u32[]{:S(2)}) collective-permute-start(f32[512,256]{1,0:T(8,128)S(1)} %broadcast_select_fusion.6), channel_id=1, source_target_pairs={{0,4},{1,5},{2,6},{3,7},{4,0},{5,1},{8,12},{9,13},{10,14},{11,15},... | collective-permute-start | bytes 1572872 | tf_op jit(solution)/shard_map/ppermute | solution.py:28
  99.0 25.3 %collective-permute-start.3 = (f32[512,256]{1,0:T(8,128)S(1)}, f32[512,256]{1,0:T(8,128)}, u32[]{:S(2)}, u32[]{:S(2)}) collective-permute-start(f32[512,256]{1,0:T(8,128)S(1)} %bitcast_multiply_fusion), channel_id=1, source_target_pairs={{0,448},{1,449},{2,450},{3,451},{4,452},{5,453},{6,454},{7,455},{8... | collective-permute-start | bytes 1572872 | tf_op jit(solution)/shard_map/ppermute | solution.py:28
  101.0 28.5 %collective-permute-start.5 = (f32[512,256]{1,0:T(8,128)S(1)}, f32[512,256]{1,0:T(8,128)S(1)}, u32[]{:S(2)}, u32[]{:S(2)}) collective-permute-start(f32[512,256]{1,0:T(8,128)S(1)} %get-tuple-element.7), channel_id=1, source_target_pairs={{0,1},{1,2},{2,3},{3,0},{4,5},{5,6},{6,7},{7,4},{8,9},{9,10},{10,1... | collective-permute-start | bytes 1572872 | tf_op jit(solution)/shard_map/ppermute | solution.py:28
  104.5 25.0 %collective-permute-start.6 = (f32[512,256]{1,0:T(8,128)S(1)}, f32[512,256]{1,0:T(8,128)S(1)}, u32[]{:S(2)}, u32[]{:S(2)}) collective-permute-start(f32[512,256]{1,0:T(8,128)S(1)} %get-tuple-element.7), channel_id=1, source_target_pairs={{0,3},{1,0},{2,1},{3,2},{4,7},{5,4},{6,5},{7,6},{8,11},{9,8},{10,9... | collective-permute-start | bytes 1572872 | tf_op jit(solution)/shard_map/ppermute | solution.py:28
  108.1 25.0 %collective-permute-start.9 = (f32[512,256]{1,0:T(8,128)S(1)}, f32[512,256]{1,0:T(8,128)}, u32[]{:S(2)}, u32[]{:S(2)}) collective-permute-start(f32[512,256]{1,0:T(8,128)S(1)} %get-tuple-element.8), channel_id=1, source_target_pairs={{0,1},{1,0},{4,5},{5,4},{8,9},{9,8},{12,13},{13,12},{16,17},{17,16... | collective-permute-start | bytes 1572872 | tf_op jit(solution)/shard_map/ppermute | solution.py:28
  126.1 8.3 %collective-permute-start.4 = (f32[512,256]{1,0:T(8,128)}, f32[512,256]{1,0:T(8,128)}, u32[]{:S(2)}, u32[]{:S(2)}) collective-permute-start(f32[512,256]{1,0:T(8,128)} %broadcast_select_fusion.4), channel_id=1, source_target_pairs={{0,32},{1,33},{2,34},{3,35},{4,36},{5,37},{6,38},{7,39},{8,40},{9,... | collective-permute-start | bytes 1572872 | tf_op jit(solution)/shard_map/ppermute | solution.py:28
  128.2 8.8 %collective-permute-start.8 = (f32[512,256]{1,0:T(8,128)S(1)}, f32[512,256]{1,0:T(8,128)S(1)}, u32[]{:S(2)}, u32[]{:S(2)}) collective-permute-start(f32[512,256]{1,0:T(8,128)S(1)} %get-tuple-element.8), channel_id=1, source_target_pairs={{0,3},{1,2},{4,7},{5,6},{8,11},{9,10},{12,15},{13,14},{16,19},{17,... | collective-permute-start | bytes 1572872 | tf_op jit(solution)/shard_map/ppermute | solution.py:28
  129.6 16.2 %collective-permute-start.7 = (f32[512,256]{1,0:T(8,128)S(1)}, f32[512,256]{1,0:T(8,128)S(1)}, u32[]{:S(2)}, u32[]{:S(2)}) collective-permute-start(f32[512,256]{1,0:T(8,128)S(1)} %broadcast_select_fusion.2), channel_id=1, source_target_pairs={{0,1},{1,0},{2,3},{3,2},{4,5},{5,4},{6,7},{7,6},{8,9},{9,8},{10,11... | collective-permute-start | bytes 1572872 | tf_op jit(solution)/shard_map/ppermute | solution.py:28
  133.1 13.9 %collective-permute-start.10 = (f32[512,256]{1,0:T(8,128)}, f32[512,256]{1,0:T(8,128)S(1)}, u32[]{:S(2)}, u32[]{:S(2)}) collective-permute-start(f32[512,256]{1,0:T(8,128)} %collective-permute-done.9), channel_id=1, source_target_pairs={{0,3},{1,2},{4,7},{5,6},{8,11},{9,10},{12,15},{13,14},{16,19},{17,... | collective-permute-start | bytes 1572872 | tf_op jit(solution)/shard_map/ppermute | solution.py:28
  148.7 54.1 %collective-permute-start.11 = (f32[512,256]{1,0:T(8,128)S(1)}, f32[512,256]{1,0:T(8,128)S(1)}, u32[]{:S(2)}, u32[]{:S(2)}) collective-permute-start(f32[512,256]{1,0:T(8,128)S(1)} %fusion.5), channel_id=1, source_target_pairs={{0,448},{1,449},{2,450},{3,451},{4,452},{5,453},{6,454},{7,455},{8... | collective-permute-start | bytes 1572872 | tf_op jit(solution)/shard_map/ppermute | solution.py:28
  202.8 3.8 %collective-permute-start.12 = (f32[512,256]{1,0:T(8,128)S(1)}, f32[512,256]{1,0:T(8,128)S(1)}, u32[]{:S(2)}, u32[]{:S(2)}) collective-permute-start(f32[512,256]{1,0:T(8,128)S(1)} %broadcast_select_fusion.3), channel_id=1, source_target_pairs={{0,32},{1,33},{2,34},{3,35},{4,36},{5,37},{6,38},{7,39},{8,40},{9,... | collective-permute-start | bytes 1572872 | tf_op jit(solution)/shard_map/ppermute | solution.py:28

commit v2 on v1

--- a/solution.py
+++ b/solution.py
@@ -86,12 +86,11 @@
     def partner(x, zh, core, zl, y):
         return x, zh, 1 - core, zl, y
 
-    def right_rows(value, anchor=None):
-        two = move(value if anchor is None else after(value, anchor), far)
+    def right_rows(value, two):
         one = move(jnp.where(core == 0, two, value), partner)
         return jnp.concatenate([value, one, two])
 
-    right = right_rows(masked, got)
+    masked_two = move(after(masked, got), far)
 
     def along(step):
         return lambda x, zh, core, zl, y: (x, zh, core, zl, (y + step) % NY)
@@ -114,6 +113,7 @@
     part_b = move(part, part_swap)
     across = move(jnp.where(y % 2 == 0, below, above), swap)
     part_c = move(part_b, part_over)
+    right = right_rows(masked, after(masked_two, (across, part_a, part_c)))
     has_part = (y // 2) == core
     part_near = jnp.where(has_part, part, part_a)
     part_far = jnp.where(has_part, part_b, part_c)
@@ -141,7 +141,7 @@
         return accum
 
     square_term = tile_mask(windowed(right), occupancy)
-    cube_term = tile_mask(windowed(right_rows(square_term)), occupancy)
+    cube_term = tile_mask(windowed(right_rows(square_term, move(square_term, far))), occupancy)
     return 3.0 * square_term - 2.0 * cube_term
 
 

time: 213 us -> 209 us (0.981)
  the two profiles are of different devices: /device:TPU:6 before, /device:TPU:1 now
where the time goes in v2:
time: 209 us
  waiting for transfers between devices  148 us (71%)
  starting transfers between devices  40.6 us (19%)
  matrix products  14.2 us (7%)
  other arithmetic  5.2 us (2%)
    ppermute x13, waiting for transfers between devices, move(): return lax.ppermute(value, ('row', 'col'), pairs)  148 us
    ppermute x13, starting transfers between devices, move(): return lax.ppermute(value, ('row', 'col'), pairs)  40.6 us
    dot_general x12, matrix products, windowed(): jnp.dot(left, rows, precision=lax.Precision.HIGHEST, preferred_element_ty...  14.2 us
  transfers between devices with their start and end apart: 13, of which 7 were waited for; matrix products, arithmetic and copies ran while one was open for 0% of the time, Pallas kernels for 0%

profile of v2, /device:TPU:1, one launch (start us, length us, event | category | flops | bytes accessed | tf_op | source)
XLA Modules:
  0.0 208.6 jit_solution(141437526022754640)
XLA Ops:
  0.0 0.7 convert_element_type.2
  0.7 0.1 copy.3
  0.8 0.2 mul.76
  1.0 1.1 bitcast_multiply_fusion
  2.1 0.7 collective-permute-start
  2.8 0.0 collective-permute-done
  2.8 0.1 broadcast_select_fusion.5
  2.9 0.7 collective-permute-start.1
  3.7 0.0 collective-permute-done.1
  3.7 0.1 broadcast_select_fusion.6
  3.8 1.3 collective-permute-start.2
  5.1 53.4 %collective-permute-done.2 = f32[512,256]{1,0:T(8,128)S(1)} collective-permute-done((f32[512,256]{1,0:T(8,128)S(1)}, f32[512,256]{1,0:T(8,128)S(1)}, u32[]{:S(2)}, u32[]{:S(2)}) %collective-permute-start.2) | collective-permute-done | bytes 524320 | tf_op jit(solution)/shard_map/ppermute | solution.py:28
  58.6 0.1 broadcast_select_fusion.7
  58.6 1.5 collective-permute-start.8
  60.1 4.6 %collective-permute-start.5 = (f32[512,256]{1,0:T(8,128)S(1)}, f32[512,256]{1,0:T(8,128)S(1)}, u32[]{:S(2)}, u32[]{:S(2)}) collective-permute-start(f32[512,256]{1,0:T(8,128)S(1)} %get-tuple-element.10), channel_id=1, source_target_pairs={{0,3},{1,0},{2,1},{3,2},{4,7},{5,4},{6,5},{7,6},{8,11},{9,8},{10,9... | collective-permute-start | bytes 1572872 | tf_op jit(solution)/shard_map/ppermute | solution.py:28
  64.7 1.9 collective-permute-start.4
  66.6 1.3 collective-permute-start.7
  67.9 8.4 %collective-permute-start.3 = (f32[512,256]{1,0:T(8,128)S(1)}, f32[512,256]{1,0:T(8,128)}, u32[]{:S(2)}, u32[]{:S(2)}) collective-permute-start(f32[512,256]{1,0:T(8,128)S(1)} %bitcast_multiply_fusion), channel_id=1, source_target_pairs={{0,448},{1,449},{2,450},{3,451},{4,452},{5,453},{6,454},{7,455},{8... | collective-permute-start | bytes 1572872 | tf_op jit(solution)/shard_map/ppermute | solution.py:28
  76.4 1.3 collective-permute-start.9
  77.7 0.0 collective-permute-done.5
  77.7 1.2 collective-permute-done.4
  78.9 0.9 broadcast_select_fusion.2
  79.8 3.5 %collective-permute-start.6 = (f32[512,256]{1,0:T(8,128)}, f32[512,256]{1,0:T(8,128)}, u32[]{:S(2)}, u32[]{:S(2)}) collective-permute-start(f32[512,256]{1,0:T(8,128)} %broadcast_select_fusion.2), channel_id=1, source_target_pairs={{0,1},{1,0},{2,3},{3,2},{4,5},{5,4},{6,7},{7,6},{8,9},{9,8},{10,11... | collective-permute-start | bytes 1572872 | tf_op jit(solution)/shard_map/ppermute | solution.py:28
  83.3 3.9 %collective-permute-done.7 = f32[512,256]{1,0:T(8,128)} collective-permute-done((f32[512,256]{1,0:T(8,128)S(1)}, f32[512,256]{1,0:T(8,128)}, u32[]{:S(2)}, u32[]{:S(2)}) %collective-permute-start.7) | collective-permute-done | bytes 524320 | tf_op jit(solution)/shard_map/ppermute | solution.py:28
  87.1 15.8 %collective-permute-done.3 = f32[512,256]{1,0:T(8,128)} collective-permute-done((f32[512,256]{1,0:T(8,128)S(1)}, f32[512,256]{1,0:T(8,128)}, u32[]{:S(2)}, u32[]{:S(2)}) %collective-permute-start.3) | collective-permute-done | bytes 524320 | tf_op jit(solution)/shard_map/ppermute | solution.py:28
  103.0 0.0 collective-permute-done.9
  103.0 0.9 broadcast_select_fusion.4
  103.8 9.4 %collective-permute-start.10 = (f32[512,256]{1,0:T(8,128)}, f32[512,256]{1,0:T(8,128)}, u32[]{:S(2)}, u32[]{:S(2)}) collective-permute-start(f32[512,256]{1,0:T(8,128)} %broadcast_select_fusion.4), channel_id=1, source_target_pairs={{0,32},{1,33},{2,34},{3,35},{4,36},{5,37},{6,38},{7,39},{8,40},{9,... | collective-permute-start | bytes 1572872 | tf_op jit(solution)/shard_map/ppermute | solution.py:28
  113.4 1.7 collective-permute-done.10
  115.1 1.3 pad_maximum_fusion
  116.4 1.6 fusion.20
  118.0 1.6 fusion.22
  119.7 0.6 fusion.24
  120.3 0.6 fusion.26
  120.9 0.6 fusion.8
  121.5 1.7 fusion.5
  123.2 4.0 %collective-permute-start.11 = (f32[512,256]{1,0:T(8,128)S(1)}, f32[512,256]{1,0:T(8,128)S(1)}, u32[]{:S(2)}, u32[]{:S(2)}) collective-permute-start(f32[512,256]{1,0:T(8,128)S(1)} %fusion.5), channel_id=1, source_target_pairs={{0,448},{1,449},{2,450},{3,451},{4,452},{5,453},{6,454},{7,455},{8... | collective-permute-start | bytes 1572872 | tf_op jit(solution)/shard_map/ppermute | solution.py:28
  127.1 69.9 %collective-permute-done.11 = f32[512,256]{1,0:T(8,128)S(1)} collective-permute-done((f32[512,256]{1,0:T(8,128)S(1)}, f32[512,256]{1,0:T(8,128)S(1)}, u32[]{:S(2)}, u32[]{:S(2)}) %collective-permute-start.11) | collective-permute-done | bytes 524320 | tf_op jit(solution)/shard_map/ppermute | solution.py:28
  197.1 0.1 broadcast_select_fusion.3
  197.1 2.1 %collective-permute-start.12 = (f32[512,256]{1,0:T(8,128)S(1)}, f32[512,256]{1,0:T(8,128)S(1)}, u32[]{:S(2)}, u32[]{:S(2)}) collective-permute-start(f32[512,256]{1,0:T(8,128)S(1)} %broadcast_select_fusion.3), channel_id=1, source_target_pairs={{0,32},{1,33},{2,34},{3,35},{4,36},{5,37},{6,38},{7,39},{8,40},{9,... | collective-permute-start | bytes 1572872 | tf_op jit(solution)/shard_map/ppermute | solution.py:28
  199.3 1.7 collective-permute-done.12
  200.9 0.1 pad_maximum_fusion.1
  201.0 1.6 fusion.10
  202.7 1.6 fusion.12
  204.3 0.6 fusion.14
  204.9 0.6 fusion.16
  205.5 0.6 fusion.4
  206.1 2.5 %multiply_subtract_fusion = f32[512,256]{1,0:T(8,128)} fusion(f32[512,256]{1,0:T(8,128)S(1)} %fusion.5, f32[64,8,2,128]{3,2,1,0:T(2,128)S(1)} %bitcast.18, f32[512,256]{1,0:T(8,128)S(1)} %fusion.4, f32[1536,256]{1,0:T(8,128)S(1)} %pad_maximum_fusion.1, s32[]{:T(128)S(6)} %select_n.181, f32[512,256]{1,0:T(8,128)} %collective-permute-done.8, ...), kind=kOutput, calls=%fused_computation.16 | convolution fusion | flops 403439616 | bytes 3407877 | tf_op jit(solution)/shard_map/dot_general | solution.py:138
  (2 shorter events, 0.0 us)
Async XLA Ops:
  2.1 0.7 collective-permute-start
  2.9 0.8 collective-permute-start.1
  3.8 54.8 %collective-permute-start.2 = (f32[512,256]{1,0:T(8,128)S(1)}, f32[512,256]{1,0:T(8,128)S(1)}, u32[]{:S(2)}, u32[]{:S(2)}) collective-permute-start(f32[512,256]{1,0:T(8,128)S(1)} %broadcast_select_fusion.6), channel_id=1, source_target_pairs={{0,4},{1,5},{2,6},{3,7},{4,0},{5,1},{8,12},{9,13},{10,14},{11,15},... | collective-permute-start | bytes 1572872 | tf_op jit(solution)/shard_map/ppermute | solution.py:28
  58.6 17.7 %collective-permute-start.8 = (f32[512,256]{1,0:T(8,128)S(1)}, f32[512,256]{1,0:T(8,128)}, u32[]{:S(2)}, u32[]{:S(2)}) collective-permute-start(f32[512,256]{1,0:T(8,128)S(1)} %get-tuple-element.9), channel_id=1, source_target_pairs={{0,1},{1,0},{4,5},{5,4},{8,9},{9,8},{12,13},{13,12},{16,17},{17,16... | collective-permute-start | bytes 1572872 | tf_op jit(solution)/shard_map/ppermute | solution.py:28
  60.1 17.6 %collective-permute-start.5 = (f32[512,256]{1,0:T(8,128)S(1)}, f32[512,256]{1,0:T(8,128)S(1)}, u32[]{:S(2)}, u32[]{:S(2)}) collective-permute-start(f32[512,256]{1,0:T(8,128)S(1)} %get-tuple-element.10), channel_id=1, source_target_pairs={{0,3},{1,0},{2,1},{3,2},{4,7},{5,4},{6,5},{7,6},{8,11},{9,8},{10,9... | collective-permute-start | bytes 1572872 | tf_op jit(solution)/shard_map/ppermute | solution.py:28
  64.7 14.3 %collective-permute-start.4 = (f32[512,256]{1,0:T(8,128)S(1)}, f32[512,256]{1,0:T(8,128)S(1)}, u32[]{:S(2)}, u32[]{:S(2)}) collective-permute-start(f32[512,256]{1,0:T(8,128)S(1)} %get-tuple-element.10), channel_id=1, source_target_pairs={{0,1},{1,2},{2,3},{3,0},{4,5},{5,6},{6,7},{7,4},{8,9},{9,10},{10,1... | collective-permute-start | bytes 1572872 | tf_op jit(solution)/shard_map/ppermute | solution.py:28
  66.6 20.5 %collective-permute-start.7 = (f32[512,256]{1,0:T(8,128)S(1)}, f32[512,256]{1,0:T(8,128)}, u32[]{:S(2)}, u32[]{:S(2)}) collective-permute-start(f32[512,256]{1,0:T(8,128)S(1)} %get-tuple-element.9), channel_id=1, source_target_pairs={{0,3},{1,2},{4,7},{5,6},{8,11},{9,10},{12,15},{13,14},{16,19},{17,... | collective-permute-start | bytes 1572872 | tf_op jit(solution)/shard_map/ppermute | solution.py:28
  67.9 35.1 %collective-permute-start.3 = (f32[512,256]{1,0:T(8,128)S(1)}, f32[512,256]{1,0:T(8,128)}, u32[]{:S(2)}, u32[]{:S(2)}) collective-permute-start(f32[512,256]{1,0:T(8,128)S(1)} %bitcast_multiply_fusion), channel_id=1, source_target_pairs={{0,448},{1,449},{2,450},{3,451},{4,452},{5,453},{6,454},{7,455},{8... | collective-permute-start | bytes 1572872 | tf_op jit(solution)/shard_map/ppermute | solution.py:28
  76.4 26.6 %collective-permute-start.9 = (f32[512,256]{1,0:T(8,128)}, f32[512,256]{1,0:T(8,128)}, u32[]{:S(2)}, u32[]{:S(2)}) collective-permute-start(f32[512,256]{1,0:T(8,128)} %collective-permute-done.8), channel_id=1, source_target_pairs={{0,3},{1,2},{4,7},{5,6},{8,11},{9,10},{12,15},{13,14},{16,19},{17,... | collective-permute-start | bytes 1572872 | tf_op jit(solution)/shard_map/ppermute | solution.py:28
  79.8 23.2 %collective-permute-start.6 = (f32[512,256]{1,0:T(8,128)}, f32[512,256]{1,0:T(8,128)}, u32[]{:S(2)}, u32[]{:S(2)}) collective-permute-start(f32[512,256]{1,0:T(8,128)} %broadcast_select_fusion.2), channel_id=1, source_target_pairs={{0,1},{1,0},{2,3},{3,2},{4,5},{5,4},{6,7},{7,6},{8,9},{9,8},{10,11... | collective-permute-start | bytes 1572872 | tf_op jit(solution)/shard_map/ppermute | solution.py:28
  103.8 11.2 %collective-permute-start.10 = (f32[512,256]{1,0:T(8,128)}, f32[512,256]{1,0:T(8,128)}, u32[]{:S(2)}, u32[]{:S(2)}) collective-permute-start(f32[512,256]{1,0:T(8,128)} %broadcast_select_fusion.4), channel_id=1, source_target_pairs={{0,32},{1,33},{2,34},{3,35},{4,36},{5,37},{6,38},{7,39},{8,40},{9,... | collective-permute-start | bytes 1572872 | tf_op jit(solution)/shard_map/ppermute | solution.py:28
  123.2 73.9 %collective-permute-start.11 = (f32[512,256]{1,0:T(8,128)S(1)}, f32[512,256]{1,0:T(8,128)S(1)}, u32[]{:S(2)}, u32[]{:S(2)}) collective-permute-start(f32[512,256]{1,0:T(8,128)S(1)} %fusion.5), channel_id=1, source_target_pairs={{0,448},{1,449},{2,450},{3,451},{4,452},{5,453},{6,454},{7,455},{8... | collective-permute-start | bytes 1572872 | tf_op jit(solution)/shard_map/ppermute | solution.py:28
  197.1 3.8 %collective-permute-start.12 = (f32[512,256]{1,0:T(8,128)S(1)}, f32[512,256]{1,0:T(8,128)S(1)}, u32[]{:S(2)}, u32[]{:S(2)}) collective-permute-start(f32[512,256]{1,0:T(8,128)S(1)} %broadcast_select_fusion.3), channel_id=1, source_target_pairs={{0,32},{1,33},{2,34},{3,35},{4,36},{5,37},{6,38},{7,39},{8,40},{9,... | collective-permute-start | bytes 1572872 | tf_op jit(solution)/shard_map/ppermute | solution.py:28

commit v3 on v2

--- a/solution.py
+++ b/solution.py
@@ -2,6 +2,7 @@
 import jax.numpy as jnp
 from jax import lax
 from jax.sharding import PartitionSpec as P
+
 
 NX, NY, NZ = 4, 4, 8
 
@@ -83,23 +84,14 @@
     def far(x, zh, core, zl, y):
         return (*prev_group(x, zh), core, zl, y)
 
-    def partner(x, zh, core, zl, y):
-        return x, zh, 1 - core, zl, y
-
-    def right_rows(value, two):
-        one = move(jnp.where(core == 0, two, value), partner)
-        return jnp.concatenate([value, one, two])
-
-    masked_two = move(after(masked, got), far)
+    def partner_of(which):
+        return lambda x, zh, core, zl, y: (x, zh, 1 - core, zl, y) if core == which else None
 
     def along(step):
         return lambda x, zh, core, zl, y: (x, zh, core, zl, (y + step) % NY)
 
     def swap(x, zh, core, zl, y):
         return x, zh, core, zl, y ^ 1
-
-    def part_out(x, zh, core, zl, y):
-        return (x, zh, core, zl, 3 - y) if y // 2 == core else None
 
     def part_swap(x, zh, core, zl, y):
         return (x, zh, core, zl, y ^ 1) if y // 2 == core else None
@@ -109,39 +101,51 @@
 
     below = move(full, along(1))
     above = move(full, along(-1))
-    part_a = move(part, part_out)
+    masked_two = move(after(masked, got), far)
     part_b = move(part, part_swap)
+    part_a = move(part, part_over)
     across = move(jnp.where(y % 2 == 0, below, above), swap)
     part_c = move(part_b, part_over)
-    right = right_rows(masked, after(masked_two, (across, part_a, part_c)))
     has_part = (y // 2) == core
     part_near = jnp.where(has_part, part, part_a)
     part_far = jnp.where(has_part, part_b, part_c)
-    near_y = jnp.where(has_part, y, 3 - y)
+    near_even = jnp.where(has_part, y, 3 - y) % 2 == 0
 
-    full_of = lambda who: who % NY + 2 * core
-    part_of = lambda who: jnp.where(core == 0, 4 + who, who - 2)
-    lefts = [
-        (full, full_of(y)),
-        (below, full_of(y + NY - 1)),
-        (above, full_of(y + 1)),
-        (across, full_of(y + 2)),
-        (part_near, part_of(near_y)),
-        (part_far, part_of(near_y ^ 1)),
-    ]
+    size = full.shape[0]
+    ring = jnp.concatenate([full, above, across, below, full, above, across])
+    ring = lax.dynamic_slice(ring, ((NY - y) % NY * size, 0), (NY * size, ring.shape[1]))
+    pair = jnp.concatenate(
+        [jnp.where(near_even, part_near, part_far), jnp.where(near_even, part_far, part_near)]
+    )
+    panel = jnp.concatenate([pair, ring, pair])
+    start = jnp.where(core == 0, 2 * size, 0)
+    panel = lax.dynamic_slice(panel, (start, 0), (6 * size, ring.shape[1]))
 
-    def windowed(right):
-        width = right.shape[1]
+    def product(section, rows):
+        width = rows.shape[1]
         accum = 0.0
-        for left, half in lefts:
-            rows = lax.dynamic_slice(right, (half * width, 0), (width, width))
+        for half in range(2):
+            left = panel[(2 * section + half) * size : (2 * section + half + 1) * size]
             accum = accum + jnp.dot(
-                left, rows, precision=lax.Precision.HIGHEST, preferred_element_type=jnp.float32
+                left,
+                rows[half * width : (half + 1) * width],
+                precision=lax.Precision.HIGHEST,
+                preferred_element_type=jnp.float32,
             )
         return accum
 
-    square_term = tile_mask(windowed(right), occupancy)
-    cube_term = tile_mask(windowed(right_rows(square_term, move(square_term, far))), occupancy)
+    def windowed(value, two, ready):
+        from_one = move(value, partner_of(1))
+        accum, from_one = lax.optimization_barrier((product(0, value), from_one))
+        two = after(two, (accum, from_one, ready))
+        from_zero = move(two, partner_of(0))
+        accum = accum + product(2, two)
+        one = jnp.where(core == 0, from_one, from_zero)
+        return accum + product(1, one)
+
+    square_term = tile_mask(windowed(masked, masked_two, (panel,)), occupancy)
+    cube_two = move(square_term, far)
+    cube_term = tile_mask(windowed(square_term, cube_two, ()), occupancy)
     return 3.0 * square_term - 2.0 * cube_term
 
 

time: 209 us -> 224 us (1.072)
  waiting for transfers between devices: 148 us -> 158 us
  local copies, waits for them, and re-layouts: 0.3 us -> 5.8 us
    ppermute x13 -> x15, waiting for transfers between devices: 148 us -> 158 us  [move(): return lax.ppermute(value, ('row', 'col'), pairs)]
    unnamed x0 -> x19, local copies, waits for them, and re-layouts: none -> 4.06 us
    ppermute x13 -> x15, starting transfers between devices: 40.6 us -> 38.5 us  [move(): return lax.ppermute(value, ('row', 'col'), pairs)]
  transfers between devices with their start and end apart: 13 -> 15, of which waited for: 7 -> 8; matrix products, arithmetic and copies ran while one was open for 0% -> 6% of each run, Pallas kernels for 0% -> 0%
where the time goes in v3:
time: 224 us; the launch traced here: 223 us
  waiting for transfers between devices  158 us (71%)
  starting transfers between devices  38.5 us (17%)
  matrix products  14.4 us (6%)
  other arithmetic  6.17 us (3%)
  local copies, waits for them, and re-layouts  5.8 us (3%)
    ppermute x15, waiting for transfers between devices, move(): return lax.ppermute(value, ('row', 'col'), pairs)  158 us
    ppermute x15, starting transfers between devices, move(): return lax.ppermute(value, ('row', 'col'), pairs)  38.5 us
    dot_general x12, matrix products, product(): jnp.dot(left, rows[half * width:(half + 1) * width], precision=lax.Precis...  14.4 us
  transfers between devices with their start and end apart: 15, of which 8 were waited for; matrix products, arithmetic and copies ran while one was open for 6% of the time, Pallas kernels for 0%

profile of v3, /device:TPU:1, one launch (start us, length us, event | category | flops | bytes accessed | tf_op | source)
XLA Modules:
  0.0 223.2 jit_solution(6182073991778507929)
XLA Ops:
  0.0 0.7 convert_element_type.2
  0.8 0.2 mul.53
  1.0 1.1 bitcast_multiply_fusion.1
  2.1 0.8 collective-permute-start
  3.1 0.7 collective-permute-start.1
  3.9 1.3 collective-permute-start.2
  5.3 53.4 %collective-permute-done.2 = f32[512,256]{1,0:T(8,128)S(1)} collective-permute-done((f32[512,256]{1,0:T(8,128)S(1)}, f32[512,256]{1,0:T(8,128)S(1)}, u32[]{:S(2)}, u32[]{:S(2)}) %collective-permute-start.2) | collective-permute-done | bytes 524320 | tf_op jit(solution)/shard_map/ppermute | solution.py:29
  58.7 1.1 constant_dynamic-update-slice_fusion.6
  59.8 3.6 %collective-permute-start.6 = (f32[512,256]{1,0:T(8,128)S(1)}, f32[512,256]{1,0:T(8,128)S(1)}, u32[]{:S(2)}, u32[]{:S(2)}) collective-permute-start(f32[512,256]{1,0:T(8,128)S(1)} %get-tuple-element.20), channel_id=1, source_target_pairs={{0,3},{1,0},{2,1},{3,2},{4,7},{5,4},{6,5},{7,6},{8,11},{9,8},{10,9... | collective-permute-start | bytes 1572872 | tf_op jit(solution)/shard_map/ppermute | solution.py:29
  63.5 1.9 collective-permute-start.7
  65.4 1.5 collective-permute-start.4
  66.9 6.9 %collective-permute-done.6 = f32[512,256]{1,0:T(8,128)S(1)} collective-permute-done((f32[512,256]{1,0:T(8,128)S(1)}, f32[512,256]{1,0:T(8,128)S(1)}, u32[]{:S(2)}, u32[]{:S(2)}) %collective-permute-start.6) | collective-permute-done | bytes 524320 | tf_op jit(solution)/shard_map/ppermute | solution.py:29
  73.8 5.0 %collective-permute-done.7 = f32[512,256]{1,0:T(8,128)S(1)} collective-permute-done((f32[512,256]{1,0:T(8,128)S(1)}, f32[512,256]{1,0:T(8,128)S(1)}, u32[]{:S(2)}, u32[]{:S(2)}) %collective-permute-start.7) | collective-permute-done | bytes 524320 | tf_op jit(solution)/shard_map/ppermute | solution.py:29
  78.8 1.0 broadcast_select_fusion.2
  79.8 1.9 collective-permute-start.8
  81.8 4.8 %collective-permute-start.9 = (f32[512,256]{1,0:T(8,128)S(1)}, f32[512,256]{1,0:T(8,128)}, u32[]{:S(2)}, u32[]{:S(2)}) collective-permute-start(f32[512,256]{1,0:T(8,128)S(1)} %bitcast_multiply_fusion.1), channel_id=1, source_target_pairs={{32,0},{33,1},{34,2},{35,3},{36,4},{37,5},{38,6},{39,7},{40,8},{41... | collective-permute-start | bytes 1572872 | tf_op jit(solution)/shard_map/ppermute | solution.py:29
  86.6 1.1 reshape.18
  87.6 1.4 broadcast_multiply_fusion.1
  89.0 1.3 collective-permute-start.3
  90.3 1.3 collective-permute-start.5
  91.7 8.4 %collective-permute-start.10 = (f32[512,256]{1,0:T(8,128)S(1)}, f32[512,256]{1,0:T(8,128)}, u32[]{:S(2)}, u32[]{:S(2)}) collective-permute-start(f32[512,256]{1,0:T(8,128)S(1)} %bitcast_multiply_fusion.1), channel_id=1, source_target_pairs={{0,448},{1,449},{2,450},{3,451},{4,452},{5,453},{6,454},{7,455},{8... | collective-permute-start | bytes 1572872 | tf_op jit(solution)/shard_map/ppermute | solution.py:29
  100.1 0.8 constant_dynamic-update-slice_fusion.4
  101.0 0.8 constant_dynamic-update-slice_fusion.3
  101.8 0.8 constant_dynamic-update-slice_fusion.2
  102.6 3.3 %collective-permute-done.5 = f32[512,256]{1,0:T(8,128)S(1)} collective-permute-done((f32[512,256]{1,0:T(8,128)}, f32[512,256]{1,0:T(8,128)S(1)}, u32[]{:S(2)}, u32[]{:S(2)}) %collective-permute-start.5) | collective-permute-done | bytes 524320 | tf_op jit(solution)/shard_map/ppermute | solution.py:29
  106.6 0.6 fusion.21
  107.2 1.4 copy-done
  108.5 0.6 convolution_add_fusion.5
  109.1 24.8 %collective-permute-done.10 = f32[512,256]{1,0:T(8,128)} collective-permute-done((f32[512,256]{1,0:T(8,128)S(1)}, f32[512,256]{1,0:T(8,128)}, u32[]{:S(2)}, u32[]{:S(2)}) %collective-permute-start.10) | collective-permute-done | bytes 524320 | tf_op jit(solution)/shard_map/ppermute | solution.py:29
  134.0 1.3 collective-permute-start.11
  135.2 1.7 fusion.15
  136.9 1.2 collective-permute-done.11
  138.2 1.6 fusion.9
  139.9 1.6 convolution_add_fusion.3
  141.5 1.7 bitcast_multiply_fusion
  143.2 3.9 %collective-permute-start.12 = (f32[512,256]{1,0:T(8,128)S(1)}, f32[512,256]{1,0:T(8,128)}, u32[]{:S(2)}, u32[]{:S(2)}) collective-permute-start(f32[512,256]{1,0:T(8,128)S(1)} %get-tuple-element.31), channel_id=1, source_target_pairs={{32,0},{33,1},{34,2},{35,3},{36,4},{37,5},{38,6},{39,7},{40,8},{41... | collective-permute-start | bytes 1572872 | tf_op jit(solution)/shard_map/ppermute | solution.py:29
  147.1 4.5 %collective-permute-start.13 = (f32[512,256]{1,0:T(8,128)S(1)}, f32[512,256]{1,0:T(8,128)S(1)}, u32[]{:S(2)}, u32[]{:S(2)}) collective-permute-start(f32[512,256]{1,0:T(8,128)S(1)} %get-tuple-element.31), channel_id=1, source_target_pairs={{0,448},{1,449},{2,450},{3,451},{4,452},{5,453},{6,454},{7,455},{8... | collective-permute-start | bytes 1572872 | tf_op jit(solution)/shard_map/ppermute | solution.py:29
  151.6 0.3 reshape.19
  151.9 0.2 broadcast_multiply_fusion
  152.2 1.8 fusion.19
  154.0 1.6 convolution_add_fusion.2
  155.6 61.1 %collective-permute-done.13 = f32[512,256]{1,0:T(8,128)S(1)} collective-permute-done((f32[512,256]{1,0:T(8,128)S(1)}, f32[512,256]{1,0:T(8,128)S(1)}, u32[]{:S(2)}, u32[]{:S(2)}) %collective-permute-start.13) | collective-permute-done | bytes 524320 | tf_op jit(solution)/shard_map/ppermute | solution.py:29
  216.7 1.3 collective-permute-start.14
  218.0 0.6 fusion.13
  218.6 1.9 collective-permute-done.14
  220.6 0.6 fusion.7
  221.2 0.6 convolution_add_fusion
  221.7 1.4 fusion.4
  (34 shorter events, 1.1 us)
Async XLA Ops:
  2.1 84.5 %copy-start.2 = (f32[512,256]{1,0:T(8,128)S(1)}, f32[512,256]{1,0:T(8,128)}, u32[]{:S(2)}) copy-start(f32[512,256]{1,0:T(8,128)} %param.2) | copy-start | bytes 1572868
  2.1 0.9 collective-permute-start
  3.1 0.8 collective-permute-start.1
  3.9 54.8 %collective-permute-start.2 = (f32[512,256]{1,0:T(8,128)S(1)}, f32[512,256]{1,0:T(8,128)S(1)}, u32[]{:S(2)}, u32[]{:S(2)}) collective-permute-start(f32[512,256]{1,0:T(8,128)S(1)} %broadcast_select_fusion.4), channel_id=1, source_target_pairs={{0,4},{1,5},{2,6},{3,7},{4,0},{5,1},{8,12},{9,13},{10,14},{11,15},... | collective-permute-start | bytes 1572872 | tf_op jit(solution)/shard_map/ppermute | solution.py:29
  59.8 20.0 %copy-start.3 = (f32[512,256]{1,0:T(8,128)}, f32[512,256]{1,0:T(8,128)S(1)}, u32[]{:S(2)}) copy-start(f32[512,256]{1,0:T(8,128)S(1)} %get-tuple-element.20) | copy-start | bytes 1572868
  59.8 14.0 %collective-permute-start.6 = (f32[512,256]{1,0:T(8,128)S(1)}, f32[512,256]{1,0:T(8,128)S(1)}, u32[]{:S(2)}, u32[]{:S(2)}) collective-permute-start(f32[512,256]{1,0:T(8,128)S(1)} %get-tuple-element.20), channel_id=1, source_target_pairs={{0,3},{1,0},{2,1},{3,2},{4,7},{5,4},{6,5},{7,6},{8,11},{9,8},{10,9... | collective-permute-start | bytes 1572872 | tf_op jit(solution)/shard_map/ppermute | solution.py:29
  63.5 15.4 %collective-permute-start.7 = (f32[512,256]{1,0:T(8,128)S(1)}, f32[512,256]{1,0:T(8,128)S(1)}, u32[]{:S(2)}, u32[]{:S(2)}) collective-permute-start(f32[512,256]{1,0:T(8,128)S(1)} %get-tuple-element.20), channel_id=1, source_target_pairs={{0,1},{1,2},{2,3},{3,0},{4,5},{5,6},{6,7},{7,4},{8,9},{9,10},{10,1... | collective-permute-start | bytes 1572872 | tf_op jit(solution)/shard_map/ppermute | solution.py:29
  65.4 24.9 %collective-permute-start.4 = (f32[512,256]{1,0:T(8,128)}, f32[512,256]{1,0:T(8,128)}, u32[]{:S(2)}, u32[]{:S(2)}) collective-permute-start(f32[512,256]{1,0:T(8,128)} %get-tuple-element.24), channel_id=1, source_target_pairs={{0,1},{1,0},{4,5},{5,4},{8,9},{9,8},{12,13},{13,12},{16,17},{17,16... | collective-permute-start | bytes 1572872 | tf_op jit(solution)/shard_map/ppermute | solution.py:29
  79.8 20.3 %collective-permute-start.8 = (f32[512,256]{1,0:T(8,128)}, f32[512,256]{1,0:T(8,128)S(1)}, u32[]{:S(2)}, u32[]{:S(2)}) collective-permute-start(f32[512,256]{1,0:T(8,128)} %get-tuple-element.29), channel_id=1, source_target_pairs={{0,1},{1,0},{2,3},{3,2},{4,5},{5,4},{6,7},{7,6},{8,9},{9,8},{10,11... | collective-permute-start | bytes 1572872 | tf_op jit(solution)/shard_map/ppermute | solution.py:29
  81.8 27.4 %collective-permute-start.9 = (f32[512,256]{1,0:T(8,128)S(1)}, f32[512,256]{1,0:T(8,128)}, u32[]{:S(2)}, u32[]{:S(2)}) collective-permute-start(f32[512,256]{1,0:T(8,128)S(1)} %bitcast_multiply_fusion.1), channel_id=1, source_target_pairs={{32,0},{33,1},{34,2},{35,3},{36,4},{37,5},{38,6},{39,7},{40,8},{41... | collective-permute-start | bytes 1572872 | tf_op jit(solution)/shard_map/ppermute | solution.py:29
  87.6 14.2 %copy-start.4 = (f32[512,256]{1,0:T(8,128)S(1)}, f32[512,256]{1,0:T(8,128)}, u32[]{:S(2)}) copy-start(f32[512,256]{1,0:T(8,128)} %copy-done.3) | copy-start | bytes 1572868
  87.6 18.3 %copy-start.5 = (f32[512,256]{1,0:T(8,128)S(1)}, f32[512,256]{1,0:T(8,128)}, u32[]{:S(2)}) copy-start(f32[512,256]{1,0:T(8,128)} %get-tuple-element.24) | copy-start | bytes 1572868
  89.0 13.6 %collective-permute-start.3 = (f32[512,256]{1,0:T(8,128)}, f32[512,256]{1,0:T(8,128)S(1)}, u32[]{:S(2)}, u32[]{:S(2)}) collective-permute-start(f32[512,256]{1,0:T(8,128)} %get-tuple-element.24), channel_id=1, source_target_pairs={{0,3},{1,2},{4,7},{5,6},{8,11},{9,10},{12,15},{13,14},{16,19},{17,... | collective-permute-start | bytes 1572872 | tf_op jit(solution)/shard_map/ppermute | solution.py:29
  90.3 15.7 %collective-permute-start.5 = (f32[512,256]{1,0:T(8,128)}, f32[512,256]{1,0:T(8,128)S(1)}, u32[]{:S(2)}, u32[]{:S(2)}) collective-permute-start(f32[512,256]{1,0:T(8,128)} %collective-permute-done.4), channel_id=1, source_target_pairs={{0,3},{1,2},{4,7},{5,6},{8,11},{9,10},{12,15},{13,14},{16,19},{17,... | collective-permute-start | bytes 1572872 | tf_op jit(solution)/shard_map/ppermute | solution.py:29
  91.7 42.3 %collective-permute-start.10 = (f32[512,256]{1,0:T(8,128)S(1)}, f32[512,256]{1,0:T(8,128)}, u32[]{:S(2)}, u32[]{:S(2)}) collective-permute-start(f32[512,256]{1,0:T(8,128)S(1)} %bitcast_multiply_fusion.1), channel_id=1, source_target_pairs={{0,448},{1,449},{2,450},{3,451},{4,452},{5,453},{6,454},{7,455},{8... | collective-permute-start | bytes 1572872 | tf_op jit(solution)/shard_map/ppermute | solution.py:29
  102.6 3.6 %copy-start.6 = (f32[3584,256]{1,0:T(8,128)S(1)}, f32[3584,256]{1,0:T(8,128)}, u32[]{:S(2)}) copy-start(f32[3584,256]{1,0:T(8,128)} %constant_dynamic-update-slice_fusion.2) | copy-start | bytes 11010052
  106.6 2.0 copy-start
  134.0 4.2 %collective-permute-start.11 = (f32[512,256]{1,0:T(8,128)}, f32[512,256]{1,0:T(8,128)S(1)}, u32[]{:S(2)}, u32[]{:S(2)}) collective-permute-start(f32[512,256]{1,0:T(8,128)} %collective-permute-done.10), channel_id=1, source_target_pairs={{0,32},{1,33},{2,34},{3,35},{4,36},{5,37},{6,38},{7,39},{8,40},{9,... | collective-permute-start | bytes 1572872 | tf_op jit(solution)/shard_map/ppermute | solution.py:29
  143.2 12.4 %collective-permute-start.12 = (f32[512,256]{1,0:T(8,128)S(1)}, f32[512,256]{1,0:T(8,128)}, u32[]{:S(2)}, u32[]{:S(2)}) collective-permute-start(f32[512,256]{1,0:T(8,128)S(1)} %get-tuple-element.31), channel_id=1, source_target_pairs={{32,0},{33,1},{34,2},{35,3},{36,4},{37,5},{38,6},{39,7},{40,8},{41... | collective-permute-start | bytes 1572872 | tf_op jit(solution)/shard_map/ppermute | solution.py:29
  147.1 69.6 %collective-permute-start.13 = (f32[512,256]{1,0:T(8,128)S(1)}, f32[512,256]{1,0:T(8,128)S(1)}, u32[]{:S(2)}, u32[]{:S(2)}) collective-permute-start(f32[512,256]{1,0:T(8,128)S(1)} %get-tuple-element.31), channel_id=1, source_target_pairs={{0,448},{1,449},{2,450},{3,451},{4,452},{5,453},{6,454},{7,455},{8... | collective-permute-start | bytes 1572872 | tf_op jit(solution)/shard_map/ppermute | solution.py:29
  151.9 66.1 %copy-start.1 = (f32[4096,256]{1,0:T(8,128)S(1)}, f32[4096,256]{1,0:T(8,128)}, u32[]{:S(2)}) copy-start(f32[4096,256]{1,0:T(8,128)} %copy-done) | copy-start | bytes 12582916
  216.7 3.8 %collective-permute-start.14 = (f32[512,256]{1,0:T(8,128)S(1)}, f32[512,256]{1,0:T(8,128)S(1)}, u32[]{:S(2)}, u32[]{:S(2)}) collective-permute-start(f32[512,256]{1,0:T(8,128)S(1)} %collective-permute-done.13), channel_id=1, source_target_pairs={{0,32},{1,33},{2,34},{3,35},{4,36},{5,37},{6,38},{7,39},{8,40},{9,... | collective-permute-start | bytes 1572872 | tf_op jit(solution)/shard_map/ppermute | solution.py:29

commit v4 on v2

v4 whole, which is shorter than its diff:
```python
import jax
import jax.numpy as jnp
from jax import lax
from jax.experimental import pallas as pl
from jax.experimental.pallas import tpu as pltpu
from jax.sharding import PartitionSpec as P


NX, NY, NZ = 4, 4, 8


def coords():
    for x in range(NX):
        for zh in range(2):
            for core in range(2):
                for zl in range(NZ):
                    for y in range(NY):
                        yield x, zh, core, zl, y


def linear(x, zh, core, zl, y):
    return ((x * 2 + zh) * 2 + core) * (NZ * NY) + zl * NY + y


def move(value, rule):
    pairs = []
    for at in coords():
        to = rule(*at)
        if to is not None:
            pairs.append((linear(*at), linear(*to)))
    return lax.ppermute(value, ("row", "col"), pairs)


def half_of(x, zh, core, zl, y):
    row = (x * 2 + zh) * 2 + core
    return (zl * NY + y - 2 * row) % (NZ * NY)


def owner(*at):
    return half_of(*at) < 6


def prev_group(x, zh):
    q = (x * 2 + zh - 1) % (2 * NX)
    return q // 2, q % 2


def tile_mask(values, occupancy):
    row_total, col_total = values.shape
    tile_rows, tile_cols = occupancy.shape
    shaped = values.reshape(tile_rows, row_total // tile_rows, tile_cols, col_total // tile_cols)
    weights = occupancy.astype(jnp.float32)[:, None, :, None]
    return (shaped * weights).reshape(row_total, col_total)


def split(value):
    high = value.astype(jnp.bfloat16)
    return high, (value - high.astype(jnp.float32)).astype(jnp.bfloat16)


def section_kernel(first, count, has_accum, finish, *refs):
    refs = list(refs)
    halves = refs.pop(0)
    occupancy = refs.pop(0) if finish else None
    rows = [refs.pop(0) for _ in range(count)]
    accum = refs.pop(0) if has_accum else None
    square = refs.pop(0) if finish == "cube" else None
    low, high, out = refs.pop(), refs.pop(), refs.pop()
    size, width = out.shape
    for index, block in enumerate(rows):
        high[index * size : (index + 1) * size], low[index * size : (index + 1) * size] = split(
            block[...]
        )
    out[...] = accum[...] if has_accum else jnp.zeros_like(out)
    for index, left in enumerate(refs):
        at = halves[index] - 2 * first

        @pl.when((at >= 0) & (at < 2 * count))
        def _():
            left_high, left_low = split(left[...])
            window = pl.ds(pl.multiple_of(at * width, width), width)
            right_high, right_low = high[window, :], low[window, :]
            dot = lambda p, q: jnp.dot(p, q, preferred_element_type=jnp.float32)
            out[...] += (dot(left_low, right_high) + dot(left_high, right_low)) + dot(
                left_high, right_high
            )

    if finish:
        tile_rows, tile_cols = size // 4, width // 2
        for i in range(4):
            for j in range(2):
                spot = (pl.ds(i * tile_rows, tile_rows), pl.ds(j * tile_cols, tile_cols))
                masked = out[spot] * occupancy[i, j].astype(jnp.float32)
                out[spot] = masked if square is None else 3.0 * square[spot] - 2.0 * masked


def section_product(lefts, halves, first, rows, accum=None, finish=None, occupancy=None, square=None):
    shape = rows[0].shape
    operands = [halves] + ([occupancy] if finish else []) + list(rows)
    operands += ([] if accum is None else [accum]) + ([square] if finish == "cube" else [])
    operands += list(lefts)
    smem = 2 if finish else 1
    in_specs = [pl.BlockSpec(memory_space=pltpu.SMEM)] * smem
    in_specs += [pl.BlockSpec(memory_space=pltpu.VMEM)] * (len(operands) - smem)
    pieces = pltpu.VMEM((len(rows) * shape[0], shape[1]), jnp.bfloat16)

    def body(*refs):
        section_kernel(first, len(rows), accum is not None, finish, *refs)

    return pl.pallas_call(
        body,
        out_shape=jax.ShapeDtypeStruct(shape, jnp.float32),
        in_specs=in_specs,
        out_specs=pl.BlockSpec(memory_space=pltpu.VMEM),
        scratch_shapes=[pieces, pieces],
        compiler_params=pltpu.CompilerParams(vmem_limit_bytes=24 << 20),
        cost_estimate=pl.CostEstimate(
            flops=len(rows) * 6 * 2 * shape[0] * shape[1] * shape[1],
            bytes_accessed=8 * shape[0] * shape[1],
            transcendentals=0,
        ),
    )(*operands)


def after(value, other):
    return lax.optimization_barrier((value, other))[0]


def per_device(density, occupancy):
    row, col = lax.axis_index("row"), lax.axis_index("col")
    core, zh = row % 2, (row // 2) % 2
    zl, y = col // NY, col % NY
    masked = tile_mask(density, occupancy)

    def from_plane(flip, known):
        def rule(x, zh, core, zl, y):
            for mask in known:
                if owner(x, zh, core, zl ^ mask, y):
                    return x, zh, core, zl ^ flip, y
            return None

        return rule

    is_owner = (col - 2 * row) % (NZ * NY) < 6
    is_owner4 = ((zl ^ 4) * NY + y - 2 * row) % (NZ * NY) < 6
    got = move(masked, from_plane(4, (0,)))
    held = jnp.where(is_owner, masked, got)
    got = move(held, from_plane(2, (0, 4)))
    held = jnp.where(is_owner | is_owner4, held, got)

    def holds_full(zh, core, zl):
        return zl % 2 == (zh + core) % 2

    def spread(value, own):
        def rule_of(full_rule, part_rule):
            def rule(x, zh, core, zl, y):
                if holds_full(zh, core, zl) == own:
                    to = full_rule(y)
                else:
                    to = part_rule(y) if y // 2 == core else None
                return None if to is None else (x, zh, core, zl, to % NY)

            return rule

        one = move(value, rule_of(lambda y: y + 1, lambda y: y ^ 1))
        two = move(value, rule_of(lambda y: y - 1, lambda y: 3 - y))
        is_full = mine_full if own else ~mine_full
        on = jnp.where(is_full & (y % 2 == 1), two, one)
        return one, two, move(on, rule_of(lambda y: y ^ 1, lambda y: 3 - y))

    def kinds(own):
        is_full = mine_full if own else ~mine_full
        as_full = [(y + step) % NY + 2 * core for step in (0, NY - 1, 1, 2)]
        has_part = (y // 2) == core
        part_of = lambda who: jnp.where(core == 0, 4 + who, who - 2)
        as_part = [
            jnp.where(has_part, part_of(y), -1),
            jnp.where(has_part, part_of(y ^ 1), -1),
            jnp.where(has_part, -1, part_of(3 - y)),
            jnp.where(has_part, -1, part_of((3 - y) ^ 1)),
        ]
        return [jnp.where(is_full, f, p) for f, p in zip(as_full, as_part)]

    mine_full = holds_full(zh, core, zl)
    got = move(held, from_plane(1, (0, 4, 2, 6)))
    own_moved = spread(held, True)

    def far(x, zh, core, zl, y):
        return (*prev_group(x, zh), core, zl, y)

    def partner_of(which):
        return lambda x, zh, core, zl, y: (x, zh, 1 - core, zl, y) if core == which else None

    masked_two = move(after(masked, got), far)
    other_moved = spread(got, False)

    lefts = [held, *own_moved, got, *other_moved]
    halves = jnp.stack(kinds(True) + kinds(False)).astype(jnp.int32)
    section = halves // 2
    early = jnp.where((section == 0) | ((core == 0) & (section == 1)), halves, -1)
    late = jnp.where((core == 1) & (section == 1), halves, -1)

    def windowed(value, two, finish, square=None):
        from_one = move(value, partner_of(1))
        accum = section_product(lefts, early, 0, [value, from_one])
        two, accum = lax.optimization_barrier((two, accum))
        from_zero = move(two, partner_of(0))
        accum = section_product(lefts, halves, 2, [two], accum)
        return section_product(lefts, late, 1, [from_zero], accum, finish, occupancy, square)

    square_term = windowed(masked, masked_two, "square")
    cube_two = move(square_term, far)
    return windowed(square_term, cube_two, "cube", square_term)


def solution(mesh):
    spec = P("row", "col")
    return jax.shard_map(
        per_device, mesh=mesh, in_specs=(spec, spec), out_specs=spec, check_vma=False
    )
```

time: 209 us -> 213 us (1.019)
  the two profiles are of different devices: /device:TPU:1 before, /device:TPU:121 now
where the time goes in v4:
time: 213 us; the launch traced here: 212 us
  waiting for transfers between devices  154 us (72%)
  starting transfers between devices  37.4 us (18%)
  Pallas kernels  14.6 us (7%)
  other arithmetic  3.49 us (2%)
  local copies, waits for them, and re-layouts  2.33 us (1%)
    ppermute x15, waiting for transfers between devices, move(): return lax.ppermute(value, ('row', 'col'), pairs)  154 us
    ppermute x15, starting transfers between devices, move(): return lax.ppermute(value, ('row', 'col'), pairs)  37.4 us
    pallas_call x6, Pallas kernels, section_product(): pl.pallas_call(body, out_shape=jax.ShapeDtypeStruct(shape, jnp.float32),...  14.6 us
  transfers between devices with their start and end apart: 15, of which 9 were waited for; matrix products, arithmetic and copies ran while one was open for 1% of the time, Pallas kernels for 4%

profile of v4, /device:TPU:121, one launch (start us, length us, event | category | flops | bytes accessed | tf_op | source)
XLA Modules:
  0.0 211.8 jit_solution(5892135002440402360)
XLA Ops:
  0.0 0.7 convert_element_type.3
  0.7 0.1 copy.3
  0.8 0.2 mul.14
  1.0 0.0 copy-done.2
  1.1 0.9 bitcast_multiply_fusion.refs_1_
  1.9 0.7 collective-permute-start
  2.6 0.0 collective-permute-done
  2.6 0.1 broadcast_select_fusion.2
  2.7 1.3 collective-permute-start.1
  4.1 43.5 %collective-permute-done.1 = f32[512,256]{1,0:T(8,128)S(1)} collective-permute-done((f32[512,256]{1,0:T(8,128)S(1)}, f32[512,256]{1,0:T(8,128)S(1)}, u32[]{:S(2)}, u32[]{:S(2)}) %collective-permute-start.1) | collective-permute-done | bytes 524320 | tf_op jit(solution)/shard_map/ppermute | solution.py:31
  47.6 0.1 broadcast_select_fusion.3.refs_3_.refs_4_.refs_5_
  47.7 1.9 collective-permute-start.2
  49.6 1.9 collective-permute-start.5
  51.5 3.4 %collective-permute-start.6 = (f32[512,256]{1,0:T(8,128)S(1)}, f32[512,256]{1,0:T(8,128)S(1)}, u32[]{:S(2)}, u32[]{:S(2)}) collective-permute-start(f32[512,256]{1,0:T(8,128)S(1)} %broadcast_select_fusion.3.refs_3_.refs_4_.refs_5_), channel_id=1, source_target_pairs={{0,3},{1,0},{2,1},{3,2},{4,7},{5,6},{8,11},{9,8},{10,9},{11,10},{1... | collective-permute-start | bytes 1572872 | tf_op jit(solution)/shard_map/ppermute | solution.py:31
  54.9 3.0 %collective-permute-done.2.refs_7_.refs_8_.refs_9_ = f32[512,256]{1,0:T(8,128)S(1)} collective-permute-done((f32[512,256]{1,0:T(8,128)S(1)}, f32[512,256]{1,0:T(8,128)S(1)}, u32[]{:S(2)}, u32[]{:S(2)}) %collective-permute-start.2) | collective-permute-done | bytes 524320 | tf_op jit(solution)/shard_map/ppermute | solution.py:31
  57.9 2.4 %collective-permute-start.8 = (f32[512,256]{1,0:T(8,128)S(1)}, f32[512,256]{1,0:T(8,128)S(1)}, u32[]{:S(2)}, u32[]{:S(2)}) collective-permute-start(f32[512,256]{1,0:T(8,128)S(1)} %collective-permute-done.2.refs_7_.refs_8_.refs_9_), channel_id=1, source_target_pairs={{0,1},{1,0},{4,5},{5,6},{6,7},{7,4},{8,9},{9,8},{12,13},{13,14},{1... | collective-permute-start | bytes 1572872 | tf_op jit(solution)/shard_map/ppermute | solution.py:31
  60.3 1.3 collective-permute-start.9
  61.6 4.8 %collective-permute-start.4 = (f32[512,256]{1,0:T(8,128)}, f32[512,256]{1,0:T(8,128)}, u32[]{:S(2)}, u32[]{:S(2)}) collective-permute-start(f32[512,256]{1,0:T(8,128)} %bitcast_multiply_fusion.refs_1_), channel_id=1, source_target_pairs={{32,0},{33,1},{34,2},{35,3},{36,4},{37,5},{38,6},{39,7},{40,8},{41... | collective-permute-start | bytes 1572872 | tf_op jit(solution)/shard_map/ppermute | solution.py:31
  66.4 0.0 collective-permute-done.5.refs_4_.refs_5_.refs_6_
  66.4 0.6 collective-permute-done.6.refs_5_.refs_6_.refs_7_
  66.9 0.9 broadcast_select_fusion.1
  67.8 2.0 collective-permute-start.7
  69.8 1.2 collective-permute-done.8.refs_8_.refs_9_.refs_10_
  71.1 1.9 collective-permute-done.9.refs_9_.refs_10_.refs_11_
  72.9 0.9 broadcast_select_fusion
  73.8 6.1 %collective-permute-start.10 = (f32[512,256]{1,0:T(8,128)}, f32[512,256]{1,0:T(8,128)}, u32[]{:S(2)}, u32[]{:S(2)}) collective-permute-start(f32[512,256]{1,0:T(8,128)} %broadcast_select_fusion), channel_id=1, source_target_pairs={{0,3},{1,2},{4,5},{5,4},{6,7},{7,6},{8,11},{9,10},{12,13},{13,12},... | collective-permute-start | bytes 1572872 | tf_op jit(solution)/shard_map/ppermute | solution.py:31
  79.9 1.9 collective-permute-start.3
  82.0 0.1 stack.35.refs_0_
  82.1 0.0 collective-permute-done.7.refs_6_.refs_7_.refs_8_
  82.1 3.5 %collective-permute-done.10.refs_10_.refs_11_.refs_12_ = f32[512,256]{1,0:T(8,128)} collective-permute-done((f32[512,256]{1,0:T(8,128)}, f32[512,256]{1,0:T(8,128)}, u32[]{:S(2)}, u32[]{:S(2)}) %collective-permute-start.10) | collective-permute-done | bytes 524320 | tf_op jit(solution)/shard_map/ppermute | solution.py:31
  85.5 2.5 %shard_map.28.refs_2_ = f32[512,256]{1,0:T(8,128)S(1)} custom-call(s32[8]{0:T(128)S(1)} %get-tuple-element.15.refs_0_, f32[512,256]{1,0:T(8,128)} %bitcast_multiply_fusion.refs_1_, f32[512,256]{1,0:T(8,128)} %collective-permute-done.4.refs_2_, f32[512,256]{1,0:T(8,128)S(1)} %broadcast_select_fusion.3.refs_3_.refs_4_.refs_5_, ...), custom_call_target="tpu_custom_call" | custom-call | flops 805306368 | bytes 1048576 | tf_op jit(solution)/shard_map/pallas_call | solution.py:110
  88.1 0.8 copy-done
  88.9 48.9 %collective-permute-done.3.refs_1_ = f32[512,256]{1,0:T(8,128)} collective-permute-done((f32[512,256]{1,0:T(8,128)}, f32[512,256]{1,0:T(8,128)}, u32[]{:S(2)}, u32[]{:S(2)}) %collective-permute-start.3) | collective-permute-done | bytes 524320 | tf_op jit(solution)/shard_map/ppermute | solution.py:31
  137.8 1.3 collective-permute-start.11
  139.1 0.1 copy.5.refs_1_
  139.2 1.0 copy-done.1
  140.3 2.3 %shard_map.29.refs_3_ = f32[512,256]{1,0:T(8,128)S(1)} custom-call(s32[8]{0:T(128)S(1)} %stack.35.refs_0_, f32[512,256]{1,0:T(8,128)} %collective-permute-done.3.refs_1_, f32[512,256]{1,0:T(8,128)S(1)} %copy-done.1, f32[512,256]{1,0:T(8,128)S(1)} %broadcast_select_fusion.3.refs_3_.refs_4_.refs_5_, ...), custom_call_target="tpu_custom_call" | custom-call | flops 402653184 | bytes 1048576 | tf_op jit(solution)/shard_map/pallas_call | solution.py:110
  142.6 0.0 collective-permute-done.11.refs_2_
  142.6 2.3 %shard_map.30.refs_1_.refs_4_ = f32[512,256]{1,0:T(8,128)S(1)} custom-call(s32[8]{0:T(128)S(1)} %and_select_fusion.refs_0_, s32[4,2]{1,0:T(4,128)S(1)} %copy.5.refs_1_, f32[512,256]{1,0:T(8,128)} %collective-permute-done.11.refs_2_, f32[512,256]{1,0:T(8,128)S(1)} %shard_map.29.refs_3_, f32[512,256]{1,0:T(8,128)S(1)} %broadcast_select_fusion.3.refs_3_.refs_4_.refs_5_, ...), custom_call_target="tpu_custom_call" | custom-call | flops 402653184 | bytes 1048576 | tf_op jit(solution)/shard_map/pallas_call | solution.py:110
  144.9 3.1 %collective-permute-start.13 = (f32[512,256]{1,0:T(8,128)S(1)}, f32[512,256]{1,0:T(8,128)S(1)}, u32[]{:S(2)}, u32[]{:S(2)}) collective-permute-start(f32[512,256]{1,0:T(8,128)S(1)} %shard_map.30.refs_1_.refs_4_), channel_id=1, source_target_pairs={{32,0},{33,1},{34,2},{35,3},{36,4},{37,5},{38,6},{39,7},{40,8},{41... | collective-permute-start | bytes 1572872 | tf_op jit(solution)/shard_map/ppermute | solution.py:31
  148.0 4.0 %collective-permute-start.12 = (f32[512,256]{1,0:T(8,128)S(1)}, f32[512,256]{1,0:T(8,128)S(1)}, u32[]{:S(2)}, u32[]{:S(2)}) collective-permute-start(f32[512,256]{1,0:T(8,128)S(1)} %shard_map.30.refs_1_.refs_4_), channel_id=1, source_target_pairs={{0,448},{1,449},{2,450},{3,451},{4,452},{5,453},{6,454},{7,455},{8... | collective-permute-start | bytes 1572872 | tf_op jit(solution)/shard_map/ppermute | solution.py:31
  152.0 0.0 collective-permute-done.13.refs_2_
  152.0 2.4 %shard_map.31.refs_2_ = f32[512,256]{1,0:T(8,128)S(1)} custom-call(s32[8]{0:T(128)S(1)} %get-tuple-element.15.refs_0_, f32[512,256]{1,0:T(8,128)S(1)} %shard_map.30.refs_1_.refs_4_, f32[512,256]{1,0:T(8,128)S(1)} %collective-permute-done.13.refs_2_, f32[512,256]{1,0:T(8,128)S(1)} %broadcast_select_fusion.3.refs_3_.refs_4_.refs_5_, ...), custom_call_target="tpu_custom_call" | custom-call | flops 805306368 | bytes 1048576 | tf_op jit(solution)/shard_map/pallas_call | solution.py:110
  154.4 50.6 %collective-permute-done.12.refs_1_ = f32[512,256]{1,0:T(8,128)S(1)} collective-permute-done((f32[512,256]{1,0:T(8,128)S(1)}, f32[512,256]{1,0:T(8,128)S(1)}, u32[]{:S(2)}, u32[]{:S(2)}) %collective-permute-start.12) | collective-permute-done | bytes 524320 | tf_op jit(solution)/shard_map/ppermute | solution.py:31
  205.0 1.3 collective-permute-start.14
  206.3 2.1 %shard_map.32.refs_3_ = f32[512,256]{1,0:T(8,128)S(1)} custom-call(s32[8]{0:T(128)S(1)} %stack.35.refs_0_, f32[512,256]{1,0:T(8,128)S(1)} %collective-permute-done.12.refs_1_, f32[512,256]{1,0:T(8,128)S(1)} %shard_map.31.refs_2_, f32[512,256]{1,0:T(8,128)S(1)} %broadcast_select_fusion.3.refs_3_.refs_4_.refs_5_, ...), custom_call_target="tpu_custom_call" | custom-call | flops 402653184 | bytes 1048576 | tf_op jit(solution)/shard_map/pallas_call | solution.py:110
  208.5 0.4 collective-permute-done.14.refs_2_
  208.8 3.0 %shard_map.33 = f32[512,256]{1,0:T(8,128)} custom-call(s32[8]{0:T(128)S(1)} %and_select_fusion.refs_0_, s32[4,2]{1,0:T(4,128)S(1)} %copy.5.refs_1_, f32[512,256]{1,0:T(8,128)S(1)} %collective-permute-done.14.refs_2_, f32[512,256]{1,0:T(8,128)S(1)} %shard_map.32.refs_3_, f32[512,256]{1,0:T(8,128)S(1)} %shard_map.30.refs_1_.refs_4_, ...), custom_call_target="tpu_custom_call" | custom-call | flops 402653184 | bytes 1048576 | tf_op jit(solution)/shard_map/pallas_call | solution.py:110
  (8 shorter events, 0.0 us)
Async XLA Ops:
  0.0 1.1 copy-start.2
  1.9 0.7 collective-permute-start
  2.7 44.9 %collective-permute-start.1 = (f32[512,256]{1,0:T(8,128)S(1)}, f32[512,256]{1,0:T(8,128)S(1)}, u32[]{:S(2)}, u32[]{:S(2)}) collective-permute-start(f32[512,256]{1,0:T(8,128)S(1)} %broadcast_select_fusion.2), channel_id=1, source_target_pairs={{0,8},{1,9},{2,10},{3,11},{4,12},{5,13},{16,24},{17,25},{18,26},{1... | collective-permute-start | bytes 1572872 | tf_op jit(solution)/shard_map/ppermute | solution.py:31
  47.7 10.2 %collective-permute-start.2 = (f32[512,256]{1,0:T(8,128)S(1)}, f32[512,256]{1,0:T(8,128)S(1)}, u32[]{:S(2)}, u32[]{:S(2)}) collective-permute-start(f32[512,256]{1,0:T(8,128)S(1)} %broadcast_select_fusion.3.refs_3_.refs_4_.refs_5_), channel_id=1, source_target_pairs={{0,4},{1,5},{2,6},{3,7},{4,0},{5,1},{8,12},{9,13},{10,14},{11,15},... | collective-permute-start | bytes 1572872 | tf_op jit(solution)/shard_map/ppermute | solution.py:31
  49.6 16.8 %collective-permute-start.5 = (f32[512,256]{1,0:T(8,128)S(1)}, f32[512,256]{1,0:T(8,128)S(1)}, u32[]{:S(2)}, u32[]{:S(2)}) collective-permute-start(f32[512,256]{1,0:T(8,128)S(1)} %broadcast_select_fusion.3.refs_3_.refs_4_.refs_5_), channel_id=1, source_target_pairs={{0,1},{1,2},{2,3},{3,0},{4,5},{5,4},{8,9},{9,10},{10,11},{11,8},{1... | collective-permute-start | bytes 1572872 | tf_op jit(solution)/shard_map/ppermute | solution.py:31
  51.5 15.4 %collective-permute-start.6 = (f32[512,256]{1,0:T(8,128)S(1)}, f32[512,256]{1,0:T(8,128)S(1)}, u32[]{:S(2)}, u32[]{:S(2)}) collective-permute-start(f32[512,256]{1,0:T(8,128)S(1)} %broadcast_select_fusion.3.refs_3_.refs_4_.refs_5_), channel_id=1, source_target_pairs={{0,3},{1,0},{2,1},{3,2},{4,7},{5,6},{8,11},{9,8},{10,9},{11,10},{1... | collective-permute-start | bytes 1572872 | tf_op jit(solution)/shard_map/ppermute | solution.py:31
  57.9 13.2 %collective-permute-start.8 = (f32[512,256]{1,0:T(8,128)S(1)}, f32[512,256]{1,0:T(8,128)S(1)}, u32[]{:S(2)}, u32[]{:S(2)}) collective-permute-start(f32[512,256]{1,0:T(8,128)S(1)} %collective-permute-done.2.refs_7_.refs_8_.refs_9_), channel_id=1, source_target_pairs={{0,1},{1,0},{4,5},{5,6},{6,7},{7,4},{8,9},{9,8},{12,13},{13,14},{1... | collective-permute-start | bytes 1572872 | tf_op jit(solution)/shard_map/ppermute | solution.py:31
  60.3 12.7 %collective-permute-start.9 = (f32[512,256]{1,0:T(8,128)S(1)}, f32[512,256]{1,0:T(8,128)S(1)}, u32[]{:S(2)}, u32[]{:S(2)}) collective-permute-start(f32[512,256]{1,0:T(8,128)S(1)} %collective-permute-done.2.refs_7_.refs_8_.refs_9_), channel_id=1, source_target_pairs={{0,3},{1,2},{4,7},{5,4},{6,5},{7,6},{8,11},{9,10},{12,15},{13,12},... | collective-permute-start | bytes 1572872 | tf_op jit(solution)/shard_map/ppermute | solution.py:31
  61.6 20.5 %collective-permute-start.4 = (f32[512,256]{1,0:T(8,128)}, f32[512,256]{1,0:T(8,128)}, u32[]{:S(2)}, u32[]{:S(2)}) collective-permute-start(f32[512,256]{1,0:T(8,128)} %bitcast_multiply_fusion.refs_1_), channel_id=1, source_target_pairs={{32,0},{33,1},{34,2},{35,3},{36,4},{37,5},{38,6},{39,7},{40,8},{41... | collective-permute-start | bytes 1572872 | tf_op jit(solution)/shard_map/ppermute | solution.py:31
  67.8 14.3 %collective-permute-start.7 = (f32[512,256]{1,0:T(8,128)}, f32[512,256]{1,0:T(8,128)}, u32[]{:S(2)}, u32[]{:S(2)}) collective-permute-start(f32[512,256]{1,0:T(8,128)} %broadcast_select_fusion.1), channel_id=1, source_target_pairs={{0,1},{1,0},{2,3},{3,2},{4,7},{5,6},{8,9},{9,8},{10,11},{11,10},{1... | collective-permute-start | bytes 1572872 | tf_op jit(solution)/shard_map/ppermute | solution.py:31
  73.8 11.7 %collective-permute-start.10 = (f32[512,256]{1,0:T(8,128)}, f32[512,256]{1,0:T(8,128)}, u32[]{:S(2)}, u32[]{:S(2)}) collective-permute-start(f32[512,256]{1,0:T(8,128)} %broadcast_select_fusion), channel_id=1, source_target_pairs={{0,3},{1,2},{4,5},{5,4},{6,7},{7,6},{8,11},{9,10},{12,13},{13,12},... | collective-permute-start | bytes 1572872 | tf_op jit(solution)/shard_map/ppermute | solution.py:31
  79.9 57.9 %collective-permute-start.3 = (f32[512,256]{1,0:T(8,128)}, f32[512,256]{1,0:T(8,128)}, u32[]{:S(2)}, u32[]{:S(2)}) collective-permute-start(f32[512,256]{1,0:T(8,128)} %bitcast_multiply_fusion.refs_1_), channel_id=1, source_target_pairs={{0,448},{1,449},{2,450},{3,451},{4,452},{5,453},{6,454},{7,455},{8... | collective-permute-start | bytes 1572872 | tf_op jit(solution)/shard_map/ppermute | solution.py:31
  88.1 0.8 copy-start
  88.9 50.2 %copy-start.3 = (s32[4,2]{0,1:T(2,128)S(1)}, s32[4,2]{0,1:T(2,128)}, u32[]{:S(2)}) copy-start(s32[4,2]{0,1:T(2,128)} %param.3) | copy-start | bytes 100
  137.8 4.7 %collective-permute-start.11 = (f32[512,256]{1,0:T(8,128)}, f32[512,256]{1,0:T(8,128)}, u32[]{:S(2)}, u32[]{:S(2)}) collective-permute-start(f32[512,256]{1,0:T(8,128)} %collective-permute-done.3.refs_1_), channel_id=1, source_target_pairs={{0,32},{1,33},{2,34},{3,35},{4,36},{5,37},{6,38},{7,39},{8,40},{9,... | collective-permute-start | bytes 1572872 | tf_op jit(solution)/shard_map/ppermute | solution.py:31
  139.2 1.0 copy-start.1
  144.9 7.1 %collective-permute-start.13 = (f32[512,256]{1,0:T(8,128)S(1)}, f32[512,256]{1,0:T(8,128)S(1)}, u32[]{:S(2)}, u32[]{:S(2)}) collective-permute-start(f32[512,256]{1,0:T(8,128)S(1)} %shard_map.30.refs_1_.refs_4_), channel_id=1, source_target_pairs={{32,0},{33,1},{34,2},{35,3},{36,4},{37,5},{38,6},{39,7},{40,8},{41... | collective-permute-start | bytes 1572872 | tf_op jit(solution)/shard_map/ppermute | solution.py:31
  148.0 57.0 %collective-permute-start.12 = (f32[512,256]{1,0:T(8,128)S(1)}, f32[512,256]{1,0:T(8,128)S(1)}, u32[]{:S(2)}, u32[]{:S(2)}) collective-permute-start(f32[512,256]{1,0:T(8,128)S(1)} %shard_map.30.refs_1_.refs_4_), channel_id=1, source_target_pairs={{0,448},{1,449},{2,450},{3,451},{4,452},{5,453},{6,454},{7,455},{8... | collective-permute-start | bytes 1572872 | tf_op jit(solution)/shard_map/ppermute | solution.py:31
  205.0 3.8 %collective-permute-start.14 = (f32[512,256]{1,0:T(8,128)S(1)}, f32[512,256]{1,0:T(8,128)S(1)}, u32[]{:S(2)}, u32[]{:S(2)}) collective-permute-start(f32[512,256]{1,0:T(8,128)S(1)} %collective-permute-done.12.refs_1_), channel_id=1, source_target_pairs={{0,32},{1,33},{2,34},{3,35},{4,36},{5,37},{6,38},{7,39},{8,40},{9,... | collective-permute-start | bytes 1572872 | tf_op jit(solution)/shard_map/ppermute | solution.py:31

commit v5 on v4

--- a/solution.py
+++ b/solution.py
@@ -113,17 +113,13 @@
         in_specs=in_specs,
         out_specs=pl.BlockSpec(memory_space=pltpu.VMEM),
         scratch_shapes=[pieces, pieces],
-        compiler_params=pltpu.CompilerParams(vmem_limit_bytes=24 << 20),
+        compiler_params=pltpu.CompilerParams(vmem_limit_bytes=6 << 20),
         cost_estimate=pl.CostEstimate(
             flops=len(rows) * 6 * 2 * shape[0] * shape[1] * shape[1],
             bytes_accessed=8 * shape[0] * shape[1],
             transcendentals=0,
         ),
     )(*operands)
-
-
-def after(value, other):
-    return lax.optimization_barrier((value, other))[0]
 
 
 def per_device(density, occupancy):
@@ -191,7 +187,7 @@
     def partner_of(which):
         return lambda x, zh, core, zl, y: (x, zh, 1 - core, zl, y) if core == which else None
 
-    masked_two = move(after(masked, got), far)
+    masked_two = move(masked, far)
     other_moved = spread(got, False)
 
     lefts = [held, *own_moved, got, *other_moved]
@@ -203,7 +199,6 @@
     def windowed(value, two, finish, square=None):
         from_one = move(value, partner_of(1))
         accum = section_product(lefts, early, 0, [value, from_one])
-        two, accum = lax.optimization_barrier((two, accum))
         from_zero = move(two, partner_of(0))
         accum = section_product(lefts, halves, 2, [two], accum)
         return section_product(lefts, late, 1, [from_zero], accum, finish, occupancy, square)

time: 213 us -> 200 us (0.939)
  the two profiles are of different devices: /device:TPU:121 before, /device:TPU:40 now
where the time goes in v5:
time: 200 us; the launch traced here: 199 us
  waiting for transfers between devices  118 us (59%)
  starting transfers between devices  60.6 us (30%)
  Pallas kernels  14.5 us (7%)
  other arithmetic  4.55 us (2%)
    ppermute x15, waiting for transfers between devices, move(): return lax.ppermute(value, ('row', 'col'), pairs)  118 us
    ppermute x15, starting transfers between devices, move(): return lax.ppermute(value, ('row', 'col'), pairs)  60.6 us
    pallas_call x6, Pallas kernels, section_product(): pl.pallas_call(body, out_shape=jax.ShapeDtypeStruct(shape, jnp.float32),...  14.5 us
  transfers between devices with their start and end apart: 15, of which 5 were waited for; matrix products, arithmetic and copies ran while one was open for 1% of the time, Pallas kernels for 5%

profile of v5, /device:TPU:40, one launch (start us, length us, event | category | flops | bytes accessed | tf_op | source)
XLA Modules:
  0.0 199.2 jit_solution(18242061442381513761)
XLA Ops:
  0.0 0.7 convert_element_type.3
  0.7 0.1 copy.3
  0.8 0.2 mul.14
  1.0 0.0 copy-done
  1.1 0.9 bitcast_multiply_fusion.refs_1_
  1.9 9.1 %collective-permute-start.3 = (f32[512,256]{1,0:T(8,128)}, f32[512,256]{1,0:T(8,128)S(1)}, u32[]{:S(2)}, u32[]{:S(2)}) collective-permute-start(f32[512,256]{1,0:T(8,128)} %bitcast_multiply_fusion.refs_1_), channel_id=1, source_target_pairs={{0,16},{1,17},{2,18},{3,19},{4,20},{5,21},{34,50},{35,51},{36,52},... | collective-permute-start | bytes 1572872 | tf_op jit(solution)/shard_map/ppermute | solution.py:31
  11.1 22.7 %collective-permute-done.3 = f32[512,256]{1,0:T(8,128)S(1)} collective-permute-done((f32[512,256]{1,0:T(8,128)}, f32[512,256]{1,0:T(8,128)S(1)}, u32[]{:S(2)}, u32[]{:S(2)}) %collective-permute-start.3) | collective-permute-done | bytes 524320 | tf_op jit(solution)/shard_map/ppermute | solution.py:31
  33.7 1.1 broadcast_select_fusion.2
  34.8 1.3 collective-permute-start.4
  36.2 10.9 %collective-permute-done.4 = f32[512,256]{1,0:T(8,128)S(1)} collective-permute-done((f32[512,256]{1,0:T(8,128)S(1)}, f32[512,256]{1,0:T(8,128)S(1)}, u32[]{:S(2)}, u32[]{:S(2)}) %collective-permute-start.4) | collective-permute-done | bytes 524320 | tf_op jit(solution)/shard_map/ppermute | solution.py:31
  47.1 0.1 broadcast_select_fusion.3.refs_3_.refs_4_.refs_5_
  47.1 1.9 collective-permute-start.8
  49.1 1.3 collective-permute-start.6
  50.4 2.4 %collective-permute-start.5 = (f32[512,256]{1,0:T(8,128)S(1)}, f32[512,256]{1,0:T(8,128)S(1)}, u32[]{:S(2)}, u32[]{:S(2)}) collective-permute-start(f32[512,256]{1,0:T(8,128)S(1)} %broadcast_select_fusion.3.refs_3_.refs_4_.refs_5_), channel_id=1, source_target_pairs={{0,1},{1,2},{2,3},{3,0},{4,5},{5,4},{8,9},{9,10},{10,11},{11,8},{1... | collective-permute-start | bytes 1572872 | tf_op jit(solution)/shard_map/ppermute | solution.py:31
  52.8 6.0 %collective-permute-done.8.refs_7_.refs_8_.refs_9_ = f32[512,256]{1,0:T(8,128)S(1)} collective-permute-done((f32[512,256]{1,0:T(8,128)S(1)}, f32[512,256]{1,0:T(8,128)S(1)}, u32[]{:S(2)}, u32[]{:S(2)}) %collective-permute-start.8) | collective-permute-done | bytes 524320 | tf_op jit(solution)/shard_map/ppermute | solution.py:31
  58.8 2.3 %collective-permute-start.10 = (f32[512,256]{1,0:T(8,128)S(1)}, f32[512,256]{1,0:T(8,128)S(1)}, u32[]{:S(2)}, u32[]{:S(2)}) collective-permute-start(f32[512,256]{1,0:T(8,128)S(1)} %collective-permute-done.8.refs_7_.refs_8_.refs_9_), channel_id=1, source_target_pairs={{0,3},{1,2},{4,7},{5,4},{6,5},{7,6},{8,11},{9,10},{12,15},{13,12},... | collective-permute-start | bytes 1572872 | tf_op jit(solution)/shard_map/ppermute | solution.py:31
  61.2 3.5 %collective-permute-start.9 = (f32[512,256]{1,0:T(8,128)S(1)}, f32[512,256]{1,0:T(8,128)S(1)}, u32[]{:S(2)}, u32[]{:S(2)}) collective-permute-start(f32[512,256]{1,0:T(8,128)S(1)} %collective-permute-done.8.refs_7_.refs_8_.refs_9_), channel_id=1, source_target_pairs={{0,1},{1,0},{4,5},{5,6},{6,7},{7,4},{8,9},{9,8},{12,13},{13,14},{1... | collective-permute-start | bytes 1572872 | tf_op jit(solution)/shard_map/ppermute | solution.py:31
  64.7 1.3 collective-permute-start.2
  66.1 0.0 collective-permute-done.6.refs_5_.refs_6_.refs_7_
  66.1 7.2 %collective-permute-start = (f32[512,256]{1,0:T(8,128)}, f32[512,256]{1,0:T(8,128)}, u32[]{:S(2)}, u32[]{:S(2)}) collective-permute-start(f32[512,256]{1,0:T(8,128)} %bitcast_multiply_fusion.refs_1_), channel_id=1, source_target_pairs={{0,448},{1,449},{2,450},{3,451},{4,452},{5,453},{6,454},{7,455},{8... | collective-permute-start | bytes 1572872 | tf_op jit(solution)/shard_map/ppermute | solution.py:31
  73.2 0.0 collective-permute-done.5.refs_4_.refs_5_.refs_6_
  73.2 0.9 broadcast_select_fusion.1
  74.1 2.1 %collective-permute-start.7 = (f32[512,256]{1,0:T(8,128)}, f32[512,256]{1,0:T(8,128)}, u32[]{:S(2)}, u32[]{:S(2)}) collective-permute-start(f32[512,256]{1,0:T(8,128)} %broadcast_select_fusion.1), channel_id=1, source_target_pairs={{0,1},{1,0},{2,3},{3,2},{4,7},{5,6},{8,9},{9,8},{10,11},{11,10},{1... | collective-permute-start | bytes 1572872 | tf_op jit(solution)/shard_map/ppermute | solution.py:31
  76.2 0.0 collective-permute-done.10.refs_9_.refs_10_.refs_11_
  76.2 0.0 collective-permute-done.9.refs_8_.refs_9_.refs_10_
  76.2 0.9 broadcast_select_fusion
  77.1 2.9 %collective-permute-start.11 = (f32[512,256]{1,0:T(8,128)}, f32[512,256]{1,0:T(8,128)}, u32[]{:S(2)}, u32[]{:S(2)}) collective-permute-start(f32[512,256]{1,0:T(8,128)} %broadcast_select_fusion), channel_id=1, source_target_pairs={{0,3},{1,2},{4,5},{5,4},{6,7},{7,6},{8,11},{9,10},{12,13},{13,12},... | collective-permute-start | bytes 1572872 | tf_op jit(solution)/shard_map/ppermute | solution.py:31
  80.1 0.0 copy-start.1
  80.1 0.7 copy-done.1
  80.8 0.1 copy.5.refs_1_
  80.9 0.1 stack.35.refs_0_
  81.0 32.4 %collective-permute-done.refs_1_ = f32[512,256]{1,0:T(8,128)} collective-permute-done((f32[512,256]{1,0:T(8,128)}, f32[512,256]{1,0:T(8,128)}, u32[]{:S(2)}, u32[]{:S(2)}) %collective-permute-start) | collective-permute-done | bytes 524320 | tf_op jit(solution)/shard_map/ppermute | solution.py:31
  113.4 2.6 %collective-permute-start.1 = (f32[512,256]{1,0:T(8,128)}, f32[512,256]{1,0:T(8,128)S(1)}, u32[]{:S(2)}, u32[]{:S(2)}) collective-permute-start(f32[512,256]{1,0:T(8,128)} %collective-permute-done.refs_1_), channel_id=1, source_target_pairs={{0,32},{1,33},{2,34},{3,35},{4,36},{5,37},{6,38},{7,39},{8,40},{9,... | collective-permute-start | bytes 1572872 | tf_op jit(solution)/shard_map/ppermute | solution.py:31
  116.0 0.0 collective-permute-done.2.refs_2_
  116.0 0.0 collective-permute-done.7.refs_6_.refs_7_.refs_8_
  116.0 0.0 collective-permute-done.11.refs_10_.refs_11_.refs_12_
  116.0 3.3 %shard_map.28.refs_2_ = f32[512,256]{1,0:T(8,128)S(1)} custom-call(s32[8]{0:T(128)S(1)} %get-tuple-element.5.refs_0_, f32[512,256]{1,0:T(8,128)} %bitcast_multiply_fusion.refs_1_, f32[512,256]{1,0:T(8,128)} %collective-permute-done.2.refs_2_, f32[512,256]{1,0:T(8,128)S(1)} %broadcast_select_fusion.3.refs_3_.refs_4_.refs_5_, ...), custom_call_target="tpu_custom_call" | custom-call | flops 805306368 | bytes 1048576 | tf_op jit(solution)/shard_map/pallas_call | solution.py:110
  119.3 2.3 %shard_map.29.refs_3_ = f32[512,256]{1,0:T(8,128)S(1)} custom-call(s32[8]{0:T(128)S(1)} %stack.35.refs_0_, f32[512,256]{1,0:T(8,128)} %collective-permute-done.refs_1_, f32[512,256]{1,0:T(8,128)S(1)} %shard_map.28.refs_2_, f32[512,256]{1,0:T(8,128)S(1)} %broadcast_select_fusion.3.refs_3_.refs_4_.refs_5_, ...), custom_call_target="tpu_custom_call" | custom-call | flops 402653184 | bytes 1048576 | tf_op jit(solution)/shard_map/pallas_call | solution.py:110
  121.6 0.0 collective-permute-done.1.refs_2_
  121.6 1.4 shard_map.30.refs_1_.refs_4_
  123.0 20.2 %collective-permute-start.12 = (f32[512,256]{1,0:T(8,128)S(1)}, f32[512,256]{1,0:T(8,128)S(1)}, u32[]{:S(2)}, u32[]{:S(2)}) collective-permute-start(f32[512,256]{1,0:T(8,128)S(1)} %shard_map.30.refs_1_.refs_4_), channel_id=1, source_target_pairs={{0,448},{1,449},{2,450},{3,451},{4,452},{5,453},{6,454},{7,455},{8... | collective-permute-start | bytes 1572872 | tf_op jit(solution)/shard_map/ppermute | solution.py:31
  143.2 1.3 collective-permute-start.14
  144.5 45.8 %collective-permute-done.12.refs_1_ = f32[512,256]{1,0:T(8,128)S(1)} collective-permute-done((f32[512,256]{1,0:T(8,128)S(1)}, f32[512,256]{1,0:T(8,128)S(1)}, u32[]{:S(2)}, u32[]{:S(2)}) %collective-permute-start.12) | collective-permute-done | bytes 524320 | tf_op jit(solution)/shard_map/ppermute | solution.py:31
  190.3 1.3 collective-permute-start.13
  191.6 0.0 collective-permute-done.14.refs_2_
  191.7 3.1 %shard_map.31.refs_2_ = f32[512,256]{1,0:T(8,128)S(1)} custom-call(s32[8]{0:T(128)S(1)} %get-tuple-element.5.refs_0_, f32[512,256]{1,0:T(8,128)S(1)} %shard_map.30.refs_1_.refs_4_, f32[512,256]{1,0:T(8,128)S(1)} %collective-permute-done.14.refs_2_, f32[512,256]{1,0:T(8,128)S(1)} %broadcast_select_fusion.3.refs_3_.refs_4_.refs_5_, ...), custom_call_target="tpu_custom_call" | custom-call | flops 805306368 | bytes 1048576 | tf_op jit(solution)/shard_map/pallas_call | solution.py:110
  194.8 2.1 %shard_map.32.refs_3_ = f32[512,256]{1,0:T(8,128)S(1)} custom-call(s32[8]{0:T(128)S(1)} %stack.35.refs_0_, f32[512,256]{1,0:T(8,128)S(1)} %collective-permute-done.12.refs_1_, f32[512,256]{1,0:T(8,128)S(1)} %shard_map.31.refs_2_, f32[512,256]{1,0:T(8,128)S(1)} %broadcast_select_fusion.3.refs_3_.refs_4_.refs_5_, ...), custom_call_target="tpu_custom_call" | custom-call | flops 402653184 | bytes 1048576 | tf_op jit(solution)/shard_map/pallas_call | solution.py:110
  197.0 2.3 %shard_map.33 = f32[512,256]{1,0:T(8,128)} custom-call(s32[8]{0:T(128)S(1)} %and_select_fusion.refs_0_, s32[4,2]{1,0:T(4,128)S(1)} %copy.5.refs_1_, f32[512,256]{1,0:T(8,128)S(1)} %collective-permute-done.13.refs_2_, f32[512,256]{1,0:T(8,128)S(1)} %shard_map.32.refs_3_, f32[512,256]{1,0:T(8,128)S(1)} %shard_map.30.refs_1_.refs_4_, ...), custom_call_target="tpu_custom_call" | custom-call | flops 402653184 | bytes 1048576 | tf_op jit(solution)/shard_map/pallas_call | solution.py:110
  (4 shorter events, 0.0 us)
Async XLA Ops:
  0.0 1.1 copy-start
  1.9 31.8 %collective-permute-start.3 = (f32[512,256]{1,0:T(8,128)}, f32[512,256]{1,0:T(8,128)S(1)}, u32[]{:S(2)}, u32[]{:S(2)}) collective-permute-start(f32[512,256]{1,0:T(8,128)} %bitcast_multiply_fusion.refs_1_), channel_id=1, source_target_pairs={{0,16},{1,17},{2,18},{3,19},{4,20},{5,21},{34,50},{35,51},{36,52},... | collective-permute-start | bytes 1572872 | tf_op jit(solution)/shard_map/ppermute | solution.py:31
  34.8 12.2 %collective-permute-start.4 = (f32[512,256]{1,0:T(8,128)S(1)}, f32[512,256]{1,0:T(8,128)S(1)}, u32[]{:S(2)}, u32[]{:S(2)}) collective-permute-start(f32[512,256]{1,0:T(8,128)S(1)} %broadcast_select_fusion.2), channel_id=1, source_target_pairs={{0,8},{1,9},{2,10},{3,11},{4,12},{5,13},{16,24},{17,25},{18,26},{1... | collective-permute-start | bytes 1572872 | tf_op jit(solution)/shard_map/ppermute | solution.py:31
  47.1 11.7 %collective-permute-start.8 = (f32[512,256]{1,0:T(8,128)S(1)}, f32[512,256]{1,0:T(8,128)S(1)}, u32[]{:S(2)}, u32[]{:S(2)}) collective-permute-start(f32[512,256]{1,0:T(8,128)S(1)} %broadcast_select_fusion.3.refs_3_.refs_4_.refs_5_), channel_id=1, source_target_pairs={{0,4},{1,5},{2,6},{3,7},{4,0},{5,1},{8,12},{9,13},{10,14},{11,15},... | collective-permute-start | bytes 1572872 | tf_op jit(solution)/shard_map/ppermute | solution.py:31
  49.1 17.0 %collective-permute-start.6 = (f32[512,256]{1,0:T(8,128)S(1)}, f32[512,256]{1,0:T(8,128)S(1)}, u32[]{:S(2)}, u32[]{:S(2)}) collective-permute-start(f32[512,256]{1,0:T(8,128)S(1)} %broadcast_select_fusion.3.refs_3_.refs_4_.refs_5_), channel_id=1, source_target_pairs={{0,3},{1,0},{2,1},{3,2},{4,7},{5,6},{8,11},{9,8},{10,9},{11,10},{1... | collective-permute-start | bytes 1572872 | tf_op jit(solution)/shard_map/ppermute | solution.py:31
  50.4 22.8 %collective-permute-start.5 = (f32[512,256]{1,0:T(8,128)S(1)}, f32[512,256]{1,0:T(8,128)S(1)}, u32[]{:S(2)}, u32[]{:S(2)}) collective-permute-start(f32[512,256]{1,0:T(8,128)S(1)} %broadcast_select_fusion.3.refs_3_.refs_4_.refs_5_), channel_id=1, source_target_pairs={{0,1},{1,2},{2,3},{3,0},{4,5},{5,4},{8,9},{9,10},{10,11},{11,8},{1... | collective-permute-start | bytes 1572872 | tf_op jit(solution)/shard_map/ppermute | solution.py:31
  58.8 17.4 %collective-permute-start.10 = (f32[512,256]{1,0:T(8,128)S(1)}, f32[512,256]{1,0:T(8,128)S(1)}, u32[]{:S(2)}, u32[]{:S(2)}) collective-permute-start(f32[512,256]{1,0:T(8,128)S(1)} %collective-permute-done.8.refs_7_.refs_8_.refs_9_), channel_id=1, source_target_pairs={{0,3},{1,2},{4,7},{5,4},{6,5},{7,6},{8,11},{9,10},{12,15},{13,12},... | collective-permute-start | bytes 1572872 | tf_op jit(solution)/shard_map/ppermute | solution.py:31
  61.2 15.1 %collective-permute-start.9 = (f32[512,256]{1,0:T(8,128)S(1)}, f32[512,256]{1,0:T(8,128)S(1)}, u32[]{:S(2)}, u32[]{:S(2)}) collective-permute-start(f32[512,256]{1,0:T(8,128)S(1)} %collective-permute-done.8.refs_7_.refs_8_.refs_9_), channel_id=1, source_target_pairs={{0,1},{1,0},{4,5},{5,6},{6,7},{7,4},{8,9},{9,8},{12,13},{13,14},{1... | collective-permute-start | bytes 1572872 | tf_op jit(solution)/shard_map/ppermute | solution.py:31
  64.7 51.3 %collective-permute-start.2 = (f32[512,256]{1,0:T(8,128)}, f32[512,256]{1,0:T(8,128)}, u32[]{:S(2)}, u32[]{:S(2)}) collective-permute-start(f32[512,256]{1,0:T(8,128)} %bitcast_multiply_fusion.refs_1_), channel_id=1, source_target_pairs={{32,0},{33,1},{34,2},{35,3},{36,4},{37,5},{38,6},{39,7},{40,8},{41... | collective-permute-start | bytes 1572872 | tf_op jit(solution)/shard_map/ppermute | solution.py:31
  66.1 47.3 %collective-permute-start = (f32[512,256]{1,0:T(8,128)}, f32[512,256]{1,0:T(8,128)}, u32[]{:S(2)}, u32[]{:S(2)}) collective-permute-start(f32[512,256]{1,0:T(8,128)} %bitcast_multiply_fusion.refs_1_), channel_id=1, source_target_pairs={{0,448},{1,449},{2,450},{3,451},{4,452},{5,453},{6,454},{7,455},{8... | collective-permute-start | bytes 1572872 | tf_op jit(solution)/shard_map/ppermute | solution.py:31
  74.1 41.9 %collective-permute-start.7 = (f32[512,256]{1,0:T(8,128)}, f32[512,256]{1,0:T(8,128)}, u32[]{:S(2)}, u32[]{:S(2)}) collective-permute-start(f32[512,256]{1,0:T(8,128)} %broadcast_select_fusion.1), channel_id=1, source_target_pairs={{0,1},{1,0},{2,3},{3,2},{4,7},{5,6},{8,9},{9,8},{10,11},{11,10},{1... | collective-permute-start | bytes 1572872 | tf_op jit(solution)/shard_map/ppermute | solution.py:31
  77.1 38.9 %collective-permute-start.11 = (f32[512,256]{1,0:T(8,128)}, f32[512,256]{1,0:T(8,128)}, u32[]{:S(2)}, u32[]{:S(2)}) collective-permute-start(f32[512,256]{1,0:T(8,128)} %broadcast_select_fusion), channel_id=1, source_target_pairs={{0,3},{1,2},{4,5},{5,4},{6,7},{7,6},{8,11},{9,10},{12,13},{13,12},... | collective-permute-start | bytes 1572872 | tf_op jit(solution)/shard_map/ppermute | solution.py:31
  80.1 0.7 copy-start.1
  113.4 8.2 %collective-permute-start.1 = (f32[512,256]{1,0:T(8,128)}, f32[512,256]{1,0:T(8,128)S(1)}, u32[]{:S(2)}, u32[]{:S(2)}) collective-permute-start(f32[512,256]{1,0:T(8,128)} %collective-permute-done.refs_1_), channel_id=1, source_target_pairs={{0,32},{1,33},{2,34},{3,35},{4,36},{5,37},{6,38},{7,39},{8,40},{9,... | collective-permute-start | bytes 1572872 | tf_op jit(solution)/shard_map/ppermute | solution.py:31
  123.0 67.3 %collective-permute-start.12 = (f32[512,256]{1,0:T(8,128)S(1)}, f32[512,256]{1,0:T(8,128)S(1)}, u32[]{:S(2)}, u32[]{:S(2)}) collective-permute-start(f32[512,256]{1,0:T(8,128)S(1)} %shard_map.30.refs_1_.refs_4_), channel_id=1, source_target_pairs={{0,448},{1,449},{2,450},{3,451},{4,452},{5,453},{6,454},{7,455},{8... | collective-permute-start | bytes 1572872 | tf_op jit(solution)/shard_map/ppermute | solution.py:31
  143.2 48.4 %collective-permute-start.14 = (f32[512,256]{1,0:T(8,128)S(1)}, f32[512,256]{1,0:T(8,128)S(1)}, u32[]{:S(2)}, u32[]{:S(2)}) collective-permute-start(f32[512,256]{1,0:T(8,128)S(1)} %shard_map.30.refs_1_.refs_4_), channel_id=1, source_target_pairs={{32,0},{33,1},{34,2},{35,3},{36,4},{37,5},{38,6},{39,7},{40,8},{41... | collective-permute-start | bytes 1572872 | tf_op jit(solution)/shard_map/ppermute | solution.py:31
  190.3 6.6 %collective-permute-start.13 = (f32[512,256]{1,0:T(8,128)S(1)}, f32[512,256]{1,0:T(8,128)S(1)}, u32[]{:S(2)}, u32[]{:S(2)}) collective-permute-start(f32[512,256]{1,0:T(8,128)S(1)} %collective-permute-done.12.refs_1_), channel_id=1, source_target_pairs={{0,32},{1,33},{2,34},{3,35},{4,36},{5,37},{6,38},{7,39},{8,40},{9,... | collective-permute-start | bytes 1572872 | tf_op jit(solution)/shard_map/ppermute | solution.py:31

commit v6 on v5

--- a/solution.py
+++ b/solution.py
@@ -65,25 +65,22 @@
     rows = [refs.pop(0) for _ in range(count)]
     accum = refs.pop(0) if has_accum else None
     square = refs.pop(0) if finish == "cube" else None
-    low, high, out = refs.pop(), refs.pop(), refs.pop()
+    right, out = refs.pop(), refs.pop()
     size, width = out.shape
     for index, block in enumerate(rows):
-        high[index * size : (index + 1) * size], low[index * size : (index + 1) * size] = split(
-            block[...]
-        )
+        for half in range(2):
+            upper, lower = split(block[half * width : (half + 1) * width])
+            for piece, part in enumerate((upper, lower, upper)):
+                right[2 * index + half, piece * width : (piece + 1) * width] = part
     out[...] = accum[...] if has_accum else jnp.zeros_like(out)
     for index, left in enumerate(refs):
         at = halves[index] - 2 * first
 
         @pl.when((at >= 0) & (at < 2 * count))
         def _():
-            left_high, left_low = split(left[...])
-            window = pl.ds(pl.multiple_of(at * width, width), width)
-            right_high, right_low = high[window, :], low[window, :]
-            dot = lambda p, q: jnp.dot(p, q, preferred_element_type=jnp.float32)
-            out[...] += (dot(left_low, right_high) + dot(left_high, right_low)) + dot(
-                left_high, right_high
-            )
+            upper, lower = split(left[...])
+            pieces = jnp.concatenate([lower, upper, upper], axis=1)
+            out[...] += jnp.dot(pieces, right[at], preferred_element_type=jnp.float32)
 
     if finish:
         tile_rows, tile_cols = size // 4, width // 2
@@ -102,7 +99,7 @@
     smem = 2 if finish else 1
     in_specs = [pl.BlockSpec(memory_space=pltpu.SMEM)] * smem
     in_specs += [pl.BlockSpec(memory_space=pltpu.VMEM)] * (len(operands) - smem)
-    pieces = pltpu.VMEM((len(rows) * shape[0], shape[1]), jnp.bfloat16)
+    pieces = pltpu.VMEM((2 * len(rows), 3 * shape[1], shape[1]), jnp.bfloat16)
 
     def body(*refs):
         section_kernel(first, len(rows), accum is not None, finish, *refs)
@@ -112,7 +109,7 @@
         out_shape=jax.ShapeDtypeStruct(shape, jnp.float32),
         in_specs=in_specs,
         out_specs=pl.BlockSpec(memory_space=pltpu.VMEM),
-        scratch_shapes=[pieces, pieces],
+        scratch_shapes=[pieces],
         compiler_params=pltpu.CompilerParams(vmem_limit_bytes=6 << 20),
         cost_estimate=pl.CostEstimate(
             flops=len(rows) * 6 * 2 * shape[0] * shape[1] * shape[1],

time: 200 us -> 200 us (level)
  no operation moved by 1% of the time
where the time goes in v6:
time: 200 us; the launch traced here: 199 us
  waiting for transfers between devices  118 us (59%)
  starting transfers between devices  60.7 us (30%)
  Pallas kernels  14.5 us (7%)
  other arithmetic  4.55 us (2%)
    ppermute x15, waiting for transfers between devices, move(): return lax.ppermute(value, ('row', 'col'), pairs)  118 us
    ppermute x15, starting transfers between devices, move(): return lax.ppermute(value, ('row', 'col'), pairs)  60.7 us
    pallas_call x6, Pallas kernels, section_product(): pl.pallas_call(body, out_shape=jax.ShapeDtypeStruct(shape, jnp.float32),...  14.5 us
  transfers between devices with their start and end apart: 15, of which 5 were waited for; matrix products, arithmetic and copies ran while one was open for 1% of the time, Pallas kernels for 5%

profile of v6, /device:TPU:40, one launch (start us, length us, event | category | flops | bytes accessed | tf_op | source)
XLA Modules:
  0.0 199.2 jit_solution(5857814997120919741)
XLA Ops:
  0.0 0.7 convert_element_type.3
  0.7 0.1 copy.3
  0.8 0.2 mul.14
  1.0 0.0 copy-done
  1.1 0.9 bitcast_multiply_fusion.refs_1_
  1.9 9.1 %collective-permute-start.3 = (f32[512,256]{1,0:T(8,128)}, f32[512,256]{1,0:T(8,128)S(1)}, u32[]{:S(2)}, u32[]{:S(2)}) collective-permute-start(f32[512,256]{1,0:T(8,128)} %bitcast_multiply_fusion.refs_1_), channel_id=1, source_target_pairs={{0,16},{1,17},{2,18},{3,19},{4,20},{5,21},{34,50},{35,51},{36,52},... | collective-permute-start | bytes 1572872 | tf_op jit(solution)/shard_map/ppermute | solution.py:31
  11.1 22.7 %collective-permute-done.3 = f32[512,256]{1,0:T(8,128)S(1)} collective-permute-done((f32[512,256]{1,0:T(8,128)}, f32[512,256]{1,0:T(8,128)S(1)}, u32[]{:S(2)}, u32[]{:S(2)}) %collective-permute-start.3) | collective-permute-done | bytes 524320 | tf_op jit(solution)/shard_map/ppermute | solution.py:31
  33.7 1.1 broadcast_select_fusion.2
  34.8 1.3 collective-permute-start.4
  36.2 10.9 %collective-permute-done.4 = f32[512,256]{1,0:T(8,128)S(1)} collective-permute-done((f32[512,256]{1,0:T(8,128)S(1)}, f32[512,256]{1,0:T(8,128)S(1)}, u32[]{:S(2)}, u32[]{:S(2)}) %collective-permute-start.4) | collective-permute-done | bytes 524320 | tf_op jit(solution)/shard_map/ppermute | solution.py:31
  47.1 0.1 broadcast_select_fusion.3.refs_3_.refs_4_.refs_5_
  47.1 1.9 collective-permute-start.8
  49.1 1.3 collective-permute-start.6
  50.4 2.4 %collective-permute-start.5 = (f32[512,256]{1,0:T(8,128)S(1)}, f32[512,256]{1,0:T(8,128)S(1)}, u32[]{:S(2)}, u32[]{:S(2)}) collective-permute-start(f32[512,256]{1,0:T(8,128)S(1)} %broadcast_select_fusion.3.refs_3_.refs_4_.refs_5_), channel_id=1, source_target_pairs={{0,1},{1,2},{2,3},{3,0},{4,5},{5,4},{8,9},{9,10},{10,11},{11,8},{1... | collective-permute-start | bytes 1572872 | tf_op jit(solution)/shard_map/ppermute | solution.py:31
  52.8 6.0 %collective-permute-done.8.refs_7_.refs_8_.refs_9_ = f32[512,256]{1,0:T(8,128)S(1)} collective-permute-done((f32[512,256]{1,0:T(8,128)S(1)}, f32[512,256]{1,0:T(8,128)S(1)}, u32[]{:S(2)}, u32[]{:S(2)}) %collective-permute-start.8) | collective-permute-done | bytes 524320 | tf_op jit(solution)/shard_map/ppermute | solution.py:31
  58.8 2.3 %collective-permute-start.10 = (f32[512,256]{1,0:T(8,128)S(1)}, f32[512,256]{1,0:T(8,128)S(1)}, u32[]{:S(2)}, u32[]{:S(2)}) collective-permute-start(f32[512,256]{1,0:T(8,128)S(1)} %collective-permute-done.8.refs_7_.refs_8_.refs_9_), channel_id=1, source_target_pairs={{0,3},{1,2},{4,7},{5,4},{6,5},{7,6},{8,11},{9,10},{12,15},{13,12},... | collective-permute-start | bytes 1572872 | tf_op jit(solution)/shard_map/ppermute | solution.py:31
  61.2 3.5 %collective-permute-start.9 = (f32[512,256]{1,0:T(8,128)S(1)}, f32[512,256]{1,0:T(8,128)S(1)}, u32[]{:S(2)}, u32[]{:S(2)}) collective-permute-start(f32[512,256]{1,0:T(8,128)S(1)} %collective-permute-done.8.refs_7_.refs_8_.refs_9_), channel_id=1, source_target_pairs={{0,1},{1,0},{4,5},{5,6},{6,7},{7,4},{8,9},{9,8},{12,13},{13,14},{1... | collective-permute-start | bytes 1572872 | tf_op jit(solution)/shard_map/ppermute | solution.py:31
  64.7 1.3 collective-permute-start.2
  66.1 0.0 collective-permute-done.6.refs_5_.refs_6_.refs_7_
  66.1 7.2 %collective-permute-start = (f32[512,256]{1,0:T(8,128)}, f32[512,256]{1,0:T(8,128)}, u32[]{:S(2)}, u32[]{:S(2)}) collective-permute-start(f32[512,256]{1,0:T(8,128)} %bitcast_multiply_fusion.refs_1_), channel_id=1, source_target_pairs={{0,448},{1,449},{2,450},{3,451},{4,452},{5,453},{6,454},{7,455},{8... | collective-permute-start | bytes 1572872 | tf_op jit(solution)/shard_map/ppermute | solution.py:31
  73.2 0.0 collective-permute-done.5.refs_4_.refs_5_.refs_6_
  73.2 0.9 broadcast_select_fusion.1
  74.1 2.1 %collective-permute-start.7 = (f32[512,256]{1,0:T(8,128)}, f32[512,256]{1,0:T(8,128)}, u32[]{:S(2)}, u32[]{:S(2)}) collective-permute-start(f32[512,256]{1,0:T(8,128)} %broadcast_select_fusion.1), channel_id=1, source_target_pairs={{0,1},{1,0},{2,3},{3,2},{4,7},{5,6},{8,9},{9,8},{10,11},{11,10},{1... | collective-permute-start | bytes 1572872 | tf_op jit(solution)/shard_map/ppermute | solution.py:31
  76.2 0.0 collective-permute-done.10.refs_9_.refs_10_.refs_11_
  76.2 0.0 collective-permute-done.9.refs_8_.refs_9_.refs_10_
  76.2 0.9 broadcast_select_fusion
  77.1 2.9 %collective-permute-start.11 = (f32[512,256]{1,0:T(8,128)}, f32[512,256]{1,0:T(8,128)}, u32[]{:S(2)}, u32[]{:S(2)}) collective-permute-start(f32[512,256]{1,0:T(8,128)} %broadcast_select_fusion), channel_id=1, source_target_pairs={{0,3},{1,2},{4,5},{5,4},{6,7},{7,6},{8,11},{9,10},{12,13},{13,12},... | collective-permute-start | bytes 1572872 | tf_op jit(solution)/shard_map/ppermute | solution.py:31
  80.1 0.0 copy-start.1
  80.1 0.7 copy-done.1
  80.8 0.1 copy.5.refs_1_
  80.9 0.1 stack.35.refs_0_
  81.0 32.4 %collective-permute-done.refs_1_ = f32[512,256]{1,0:T(8,128)} collective-permute-done((f32[512,256]{1,0:T(8,128)}, f32[512,256]{1,0:T(8,128)}, u32[]{:S(2)}, u32[]{:S(2)}) %collective-permute-start) | collective-permute-done | bytes 524320 | tf_op jit(solution)/shard_map/ppermute | solution.py:31
  113.4 2.6 %collective-permute-start.1 = (f32[512,256]{1,0:T(8,128)}, f32[512,256]{1,0:T(8,128)S(1)}, u32[]{:S(2)}, u32[]{:S(2)}) collective-permute-start(f32[512,256]{1,0:T(8,128)} %collective-permute-done.refs_1_), channel_id=1, source_target_pairs={{0,32},{1,33},{2,34},{3,35},{4,36},{5,37},{6,38},{7,39},{8,40},{9,... | collective-permute-start | bytes 1572872 | tf_op jit(solution)/shard_map/ppermute | solution.py:31
  116.0 0.0 collective-permute-done.2.refs_2_
  116.0 0.0 collective-permute-done.7.refs_6_.refs_7_.refs_8_
  116.0 0.0 collective-permute-done.11.refs_10_.refs_11_.refs_12_
  116.0 3.3 %shard_map.28.refs_2_ = f32[512,256]{1,0:T(8,128)S(1)} custom-call(s32[8]{0:T(128)S(1)} %get-tuple-element.5.refs_0_, f32[512,256]{1,0:T(8,128)} %bitcast_multiply_fusion.refs_1_, f32[512,256]{1,0:T(8,128)} %collective-permute-done.2.refs_2_, f32[512,256]{1,0:T(8,128)S(1)} %broadcast_select_fusion.3.refs_3_.refs_4_.refs_5_, ...), custom_call_target="tpu_custom_call" | custom-call | flops 805306368 | bytes 1048576 | tf_op jit(solution)/shard_map/pallas_call | solution.py:107
  119.3 2.3 %shard_map.29.refs_3_ = f32[512,256]{1,0:T(8,128)S(1)} custom-call(s32[8]{0:T(128)S(1)} %stack.35.refs_0_, f32[512,256]{1,0:T(8,128)} %collective-permute-done.refs_1_, f32[512,256]{1,0:T(8,128)S(1)} %shard_map.28.refs_2_, f32[512,256]{1,0:T(8,128)S(1)} %broadcast_select_fusion.3.refs_3_.refs_4_.refs_5_, ...), custom_call_target="tpu_custom_call" | custom-call | flops 402653184 | bytes 1048576 | tf_op jit(solution)/shard_map/pallas_call | solution.py:107
  121.6 0.0 collective-permute-done.1.refs_2_
  121.6 1.4 shard_map.30.refs_1_.refs_4_
  123.0 20.2 %collective-permute-start.12 = (f32[512,256]{1,0:T(8,128)S(1)}, f32[512,256]{1,0:T(8,128)S(1)}, u32[]{:S(2)}, u32[]{:S(2)}) collective-permute-start(f32[512,256]{1,0:T(8,128)S(1)} %shard_map.30.refs_1_.refs_4_), channel_id=1, source_target_pairs={{0,448},{1,449},{2,450},{3,451},{4,452},{5,453},{6,454},{7,455},{8... | collective-permute-start | bytes 1572872 | tf_op jit(solution)/shard_map/ppermute | solution.py:31
  143.2 1.3 collective-permute-start.14
  144.5 45.8 %collective-permute-done.12.refs_1_ = f32[512,256]{1,0:T(8,128)S(1)} collective-permute-done((f32[512,256]{1,0:T(8,128)S(1)}, f32[512,256]{1,0:T(8,128)S(1)}, u32[]{:S(2)}, u32[]{:S(2)}) %collective-permute-start.12) | collective-permute-done | bytes 524320 | tf_op jit(solution)/shard_map/ppermute | solution.py:31
  190.3 1.3 collective-permute-start.13
  191.7 0.0 collective-permute-done.14.refs_2_
  191.7 3.2 %shard_map.31.refs_2_ = f32[512,256]{1,0:T(8,128)S(1)} custom-call(s32[8]{0:T(128)S(1)} %get-tuple-element.5.refs_0_, f32[512,256]{1,0:T(8,128)S(1)} %shard_map.30.refs_1_.refs_4_, f32[512,256]{1,0:T(8,128)S(1)} %collective-permute-done.14.refs_2_, f32[512,256]{1,0:T(8,128)S(1)} %broadcast_select_fusion.3.refs_3_.refs_4_.refs_5_, ...), custom_call_target="tpu_custom_call" | custom-call | flops 805306368 | bytes 1048576 | tf_op jit(solution)/shard_map/pallas_call | solution.py:107
  194.8 2.1 %shard_map.32.refs_3_ = f32[512,256]{1,0:T(8,128)S(1)} custom-call(s32[8]{0:T(128)S(1)} %stack.35.refs_0_, f32[512,256]{1,0:T(8,128)S(1)} %collective-permute-done.12.refs_1_, f32[512,256]{1,0:T(8,128)S(1)} %shard_map.31.refs_2_, f32[512,256]{1,0:T(8,128)S(1)} %broadcast_select_fusion.3.refs_3_.refs_4_.refs_5_, ...), custom_call_target="tpu_custom_call" | custom-call | flops 402653184 | bytes 1048576 | tf_op jit(solution)/shard_map/pallas_call | solution.py:107
  197.0 2.3 %shard_map.33 = f32[512,256]{1,0:T(8,128)} custom-call(s32[8]{0:T(128)S(1)} %and_select_fusion.refs_0_, s32[4,2]{1,0:T(4,128)S(1)} %copy.5.refs_1_, f32[512,256]{1,0:T(8,128)S(1)} %collective-permute-done.13.refs_2_, f32[512,256]{1,0:T(8,128)S(1)} %shard_map.32.refs_3_, f32[512,256]{1,0:T(8,128)S(1)} %shard_map.30.refs_1_.refs_4_, ...), custom_call_target="tpu_custom_call" | custom-call | flops 402653184 | bytes 1048576 | tf_op jit(solution)/shard_map/pallas_call | solution.py:107
  (4 shorter events, 0.0 us)
Async XLA Ops:
  0.0 1.1 copy-start
  1.9 31.8 %collective-permute-start.3 = (f32[512,256]{1,0:T(8,128)}, f32[512,256]{1,0:T(8,128)S(1)}, u32[]{:S(2)}, u32[]{:S(2)}) collective-permute-start(f32[512,256]{1,0:T(8,128)} %bitcast_multiply_fusion.refs_1_), channel_id=1, source_target_pairs={{0,16},{1,17},{2,18},{3,19},{4,20},{5,21},{34,50},{35,51},{36,52},... | collective-permute-start | bytes 1572872 | tf_op jit(solution)/shard_map/ppermute | solution.py:31
  34.8 12.2 %collective-permute-start.4 = (f32[512,256]{1,0:T(8,128)S(1)}, f32[512,256]{1,0:T(8,128)S(1)}, u32[]{:S(2)}, u32[]{:S(2)}) collective-permute-start(f32[512,256]{1,0:T(8,128)S(1)} %broadcast_select_fusion.2), channel_id=1, source_target_pairs={{0,8},{1,9},{2,10},{3,11},{4,12},{5,13},{16,24},{17,25},{18,26},{1... | collective-permute-start | bytes 1572872 | tf_op jit(solution)/shard_map/ppermute | solution.py:31
  47.1 11.7 %collective-permute-start.8 = (f32[512,256]{1,0:T(8,128)S(1)}, f32[512,256]{1,0:T(8,128)S(1)}, u32[]{:S(2)}, u32[]{:S(2)}) collective-permute-start(f32[512,256]{1,0:T(8,128)S(1)} %broadcast_select_fusion.3.refs_3_.refs_4_.refs_5_), channel_id=1, source_target_pairs={{0,4},{1,5},{2,6},{3,7},{4,0},{5,1},{8,12},{9,13},{10,14},{11,15},... | collective-permute-start | bytes 1572872 | tf_op jit(solution)/shard_map/ppermute | solution.py:31
  49.1 17.0 %collective-permute-start.6 = (f32[512,256]{1,0:T(8,128)S(1)}, f32[512,256]{1,0:T(8,128)S(1)}, u32[]{:S(2)}, u32[]{:S(2)}) collective-permute-start(f32[512,256]{1,0:T(8,128)S(1)} %broadcast_select_fusion.3.refs_3_.refs_4_.refs_5_), channel_id=1, source_target_pairs={{0,3},{1,0},{2,1},{3,2},{4,7},{5,6},{8,11},{9,8},{10,9},{11,10},{1... | collective-permute-start | bytes 1572872 | tf_op jit(solution)/shard_map/ppermute | solution.py:31
  50.4 22.8 %collective-permute-start.5 = (f32[512,256]{1,0:T(8,128)S(1)}, f32[512,256]{1,0:T(8,128)S(1)}, u32[]{:S(2)}, u32[]{:S(2)}) collective-permute-start(f32[512,256]{1,0:T(8,128)S(1)} %broadcast_select_fusion.3.refs_3_.refs_4_.refs_5_), channel_id=1, source_target_pairs={{0,1},{1,2},{2,3},{3,0},{4,5},{5,4},{8,9},{9,10},{10,11},{11,8},{1... | collective-permute-start | bytes 1572872 | tf_op jit(solution)/shard_map/ppermute | solution.py:31
  58.8 17.4 %collective-permute-start.10 = (f32[512,256]{1,0:T(8,128)S(1)}, f32[512,256]{1,0:T(8,128)S(1)}, u32[]{:S(2)}, u32[]{:S(2)}) collective-permute-start(f32[512,256]{1,0:T(8,128)S(1)} %collective-permute-done.8.refs_7_.refs_8_.refs_9_), channel_id=1, source_target_pairs={{0,3},{1,2},{4,7},{5,4},{6,5},{7,6},{8,11},{9,10},{12,15},{13,12},... | collective-permute-start | bytes 1572872 | tf_op jit(solution)/shard_map/ppermute | solution.py:31
  61.2 15.1 %collective-permute-start.9 = (f32[512,256]{1,0:T(8,128)S(1)}, f32[512,256]{1,0:T(8,128)S(1)}, u32[]{:S(2)}, u32[]{:S(2)}) collective-permute-start(f32[512,256]{1,0:T(8,128)S(1)} %collective-permute-done.8.refs_7_.refs_8_.refs_9_), channel_id=1, source_target_pairs={{0,1},{1,0},{4,5},{5,6},{6,7},{7,4},{8,9},{9,8},{12,13},{13,14},{1... | collective-permute-start | bytes 1572872 | tf_op jit(solution)/shard_map/ppermute | solution.py:31
  64.7 51.3 %collective-permute-start.2 = (f32[512,256]{1,0:T(8,128)}, f32[512,256]{1,0:T(8,128)}, u32[]{:S(2)}, u32[]{:S(2)}) collective-permute-start(f32[512,256]{1,0:T(8,128)} %bitcast_multiply_fusion.refs_1_), channel_id=1, source_target_pairs={{32,0},{33,1},{34,2},{35,3},{36,4},{37,5},{38,6},{39,7},{40,8},{41... | collective-permute-start | bytes 1572872 | tf_op jit(solution)/shard_map/ppermute | solution.py:31
  66.1 47.3 %collective-permute-start = (f32[512,256]{1,0:T(8,128)}, f32[512,256]{1,0:T(8,128)}, u32[]{:S(2)}, u32[]{:S(2)}) collective-permute-start(f32[512,256]{1,0:T(8,128)} %bitcast_multiply_fusion.refs_1_), channel_id=1, source_target_pairs={{0,448},{1,449},{2,450},{3,451},{4,452},{5,453},{6,454},{7,455},{8... | collective-permute-start | bytes 1572872 | tf_op jit(solution)/shard_map/ppermute | solution.py:31
  74.1 41.9 %collective-permute-start.7 = (f32[512,256]{1,0:T(8,128)}, f32[512,256]{1,0:T(8,128)}, u32[]{:S(2)}, u32[]{:S(2)}) collective-permute-start(f32[512,256]{1,0:T(8,128)} %broadcast_select_fusion.1), channel_id=1, source_target_pairs={{0,1},{1,0},{2,3},{3,2},{4,7},{5,6},{8,9},{9,8},{10,11},{11,10},{1... | collective-permute-start | bytes 1572872 | tf_op jit(solution)/shard_map/ppermute | solution.py:31
  77.1 38.9 %collective-permute-start.11 = (f32[512,256]{1,0:T(8,128)}, f32[512,256]{1,0:T(8,128)}, u32[]{:S(2)}, u32[]{:S(2)}) collective-permute-start(f32[512,256]{1,0:T(8,128)} %broadcast_select_fusion), channel_id=1, source_target_pairs={{0,3},{1,2},{4,5},{5,4},{6,7},{7,6},{8,11},{9,10},{12,13},{13,12},... | collective-permute-start | bytes 1572872 | tf_op jit(solution)/shard_map/ppermute | solution.py:31
  80.1 0.7 copy-start.1
  113.4 8.2 %collective-permute-start.1 = (f32[512,256]{1,0:T(8,128)}, f32[512,256]{1,0:T(8,128)S(1)}, u32[]{:S(2)}, u32[]{:S(2)}) collective-permute-start(f32[512,256]{1,0:T(8,128)} %collective-permute-done.refs_1_), channel_id=1, source_target_pairs={{0,32},{1,33},{2,34},{3,35},{4,36},{5,37},{6,38},{7,39},{8,40},{9,... | collective-permute-start | bytes 1572872 | tf_op jit(solution)/shard_map/ppermute | solution.py:31
  123.0 67.3 %collective-permute-start.12 = (f32[512,256]{1,0:T(8,128)S(1)}, f32[512,256]{1,0:T(8,128)S(1)}, u32[]{:S(2)}, u32[]{:S(2)}) collective-permute-start(f32[512,256]{1,0:T(8,128)S(1)} %shard_map.30.refs_1_.refs_4_), channel_id=1, source_target_pairs={{0,448},{1,449},{2,450},{3,451},{4,452},{5,453},{6,454},{7,455},{8... | collective-permute-start | bytes 1572872 | tf_op jit(solution)/shard_map/ppermute | solution.py:31
  143.2 48.4 %collective-permute-start.14 = (f32[512,256]{1,0:T(8,128)S(1)}, f32[512,256]{1,0:T(8,128)S(1)}, u32[]{:S(2)}, u32[]{:S(2)}) collective-permute-start(f32[512,256]{1,0:T(8,128)S(1)} %shard_map.30.refs_1_.refs_4_), channel_id=1, source_target_pairs={{32,0},{33,1},{34,2},{35,3},{36,4},{37,5},{38,6},{39,7},{40,8},{41... | collective-permute-start | bytes 1572872 | tf_op jit(solution)/shard_map/ppermute | solution.py:31
  190.3 6.6 %collective-permute-start.13 = (f32[512,256]{1,0:T(8,128)S(1)}, f32[512,256]{1,0:T(8,128)S(1)}, u32[]{:S(2)}, u32[]{:S(2)}) collective-permute-start(f32[512,256]{1,0:T(8,128)S(1)} %collective-permute-done.12.refs_1_), channel_id=1, source_target_pairs={{0,32},{1,33},{2,34},{3,35},{4,36},{5,37},{6,38},{7,39},{8,40},{9,... | collective-permute-start | bytes 1572872 | tf_op jit(solution)/shard_map/ppermute | solution.py:31
